TPU v7x, 32 devices: a whole 2x2x4 slice. The times are simulated.
32 devices in a mesh: seq: 2 (over x), mp: 16 (over z, y, core).
Axes of the slice: x: 2, y: 2, z: 4, core: 2. Of those that a mesh axis runs over, the one named last changes fastest.
Arguments:
- tokens: bfloat16 [4096, 2048], P(('seq', 'mp')), may hold values from -6 to 6
- lengths: int32 [2, 3], P('seq'), may hold values from 1 to 1536, 2048 in all within a row
- norm_gains: float32 [2, 2048], replicated, may hold values from 0.5 to 1.5
- norm_biases: float32 [2, 2048], replicated, may hold values from -2 to 2
- w_query: bfloat16 [2048, 2048], P(None, 'mp'), may hold values from -0.125 to 0.125
- w_key: bfloat16 [2048, 2048], P(None, 'mp'), may hold values from -0.125 to 0.125
- w_value: bfloat16 [2048, 4096], P(None, 'mp'), may hold values from -0.125 to 0.125
- w_gate: bfloat16 [2048, 4096], P(None, 'mp'), may hold values from -0.125 to 0.125
- w_out: bfloat16 [4096, 2048], P('mp'), may hold values from -0.125 to 0.125
- w_up: bfloat16 [2048, 4096], P(None, 'mp'), may hold values from -0.125 to 0.125
- w_down: bfloat16 [4096, 2048], P('mp'), may hold values from -0.125 to 0.125
- out_grad: bfloat16 [4096, 2048], P(('seq', 'mp')), may hold values from -6 to 6
Outputs:
- layer_out: float32 [4096, 2048], P(('seq', 'mp'))
- tokens_grad: float32 [4096, 2048], P(('seq', 'mp'))
- query_grad: float32 [2048, 2048], P(None, 'mp')
- key_grad: float32 [2048, 2048], P(None, 'mp')
- value_grad: float32 [2048, 4096], P(None, 'mp')
- gate_grad: float32 [2048, 4096], P(None, 'mp')
- out_weight_grad: float32 [4096, 2048], P('mp')
- up_grad: float32 [2048, 4096], P(None, 'mp')
- down_grad: float32 [4096, 2048], P('mp')
- gains_grad: float32 [2, 2048], P(None, 'mp')
- biases_grad: float32 [2, 2048], P(None, 'mp')
Inputs may be any that keep to these rules, and one draw needn't show every extreme that they name: Each row of lengths lists the 3 sequences of one group in order; they sum to 2048 and the longest is exactly 1536.
All inputs are finite; a program needn't handle non-finite values.
Results may differ from a plain program's by a relative error of at most 0.017.
Values may be sent and summed in bfloat16 or wider, within the bound.
No kernel may reach another device: no remote copies, remote signals or barrier semaphores. Data moves between devices by JAX's collectives and lax.ppermute only.
A program may use at most 576 MiB of HBM per device.

v0:
```python
import functools

import jax
import jax.numpy as jnp
import numpy as np
from jax import lax
from jax.experimental import pallas as pl
from jax.experimental.pallas import tpu as pltpu
from jax.sharding import PartitionSpec as P

HEADS = 8
KEY = 256
VAL = 512
QKV = 2 * KEY + VAL
VMEM_BYTES = 56 << 20
SPARE_BYTES = 12 << 20

epsilon = 1e-05
group_epsilon = 0.25
key_scale = KEY ** (-0.5)
bf16, f32 = jnp.bfloat16, jnp.float32

RING = tuple(range(0, HEADS, 2)) + tuple(range(HEADS - 1, 0, -2))
BATCHES = ((0, -1, 1, -2, 2), (-3, 3), (4,))
OFFSETS = tuple(offset for batch in BATCHES for offset in batch)
FIRST = (0, 5, 7)


def contract(left_side, right_side, left_dim, right_dim):
    return lax.dot_general(
        left_side,
        right_side,
        (((left_dim,), (right_dim,)), ((), ())),
        preferred_element_type=f32,
    )


def after(value, *earlier):
    return lax.optimization_barrier((value, *earlier))[0]


def row_stats(values):
    average = jnp.mean(values, axis=-1, keepdims=True)
    centered = values - average
    variance = jnp.mean(centered * centered, axis=-1, keepdims=True)
    return average, lax.rsqrt(variance + epsilon)


def normalize_back(grad_normed, unit_rows, inverse, norm_gain):
    scaled = grad_normed * norm_gain
    plain_mean = jnp.mean(scaled, axis=-1, keepdims=True)
    cross_mean = jnp.mean(scaled * unit_rows, axis=-1, keepdims=True)
    return inverse * (scaled - plain_mean - unit_rows * cross_mean)


def turn(values, cosine, sine):
    half = values.shape[-1] // 2
    even, odd = values[:, :half], values[:, half:]
    return jnp.concatenate([even * cosine - odd * sine, even * sine + odd * cosine], axis=1)


def sigmoid(values):
    return 1.0 / (1.0 + jnp.exp(-values))


def run(body, name, outs, scratch, *groups, late=(), flops=0, free=False):
    lists = [list(group) if isinstance(group, (list, tuple)) else [group] for group in groups]
    sizes = [len(group) for group in lists]
    values = [value for group in lists for value in group]
    fixed = len(outs) + len(scratch)

    def kernel(*refs):
        split, at = [], 0
        for size in sizes:
            split.append(refs[at : at + size])
            at += size
        sources = refs[at : at + len(late)]
        at += len(late)
        results = refs[at : at + fixed]
        at += fixed
        copies = [
            pltpu.make_async_copy(source, refs[at + i], refs[at + len(late) + i])
            for i, source in enumerate(sources)
        ]
        for copy in copies:
            copy.start()

        def fetch(i):
            def wait():
                copies[i].wait()
                return refs[at + i]

            return wait

        body(*split, *results, *[fetch(i) for i in range(len(late))])

    whole = pl.BlockSpec(memory_space=pltpu.VMEM)
    moved = sum(value.size * value.dtype.itemsize for value in (*values, *late))
    moved += sum(int(np.prod(shape)) * jnp.dtype(dtype).itemsize for shape, dtype in outs)
    held = sum(int(np.prod(shape)) * jnp.dtype(dtype).itemsize for shape, dtype in scratch)
    return pl.pallas_call(
        kernel,
        out_shape=[jax.ShapeDtypeStruct(shape, dtype) for shape, dtype in outs],
        in_specs=[whole] * len(values) + [pl.BlockSpec(memory_space=pl.ANY)] * len(late),
        out_specs=[whole] * len(outs),
        scratch_shapes=[pltpu.VMEM(shape, dtype) for shape, dtype in scratch]
        + [pltpu.VMEM(value.shape, value.dtype) for value in late]
        + [pltpu.SemaphoreType.DMA(())] * len(late),
        compiler_params=pltpu.CompilerParams(vmem_limit_bytes=min(VMEM_BYTES, moved + held + SPARE_BYTES)),
        cost_estimate=pl.CostEstimate(flops=flops, transcendentals=0, bytes_accessed=0 if free else moved),
        name=name,
    )(*values, *late)


def each_block(count, block, step):
    def body(i, unused):
        step(pl.multiple_of(i * block, block))
        return unused

    lax.fori_loop(0, count // block, body, 0)


def stage_rows(pieces, rows):
    width = rows.shape[1]
    half = pieces[0].shape[1]
    if half < width:
        rows[:, :half] = pieces[0][...]
        rows[:, half:] = pieces[1][...]
    else:
        chunk = rows.shape[0] // len(pieces)
        for at, piece in enumerate(pieces):
            rows[at * chunk : (at + 1) * chunk, :] = piece[...]


def project_body(pieces, norm, angles, tokens, normed, qkv, gate, stats, weights):
    (norm,), (angles,) = norm, angles
    stage_rows(pieces, tokens)
    count, width = normed.shape

    def normalize(first):
        span = pl.ds(first, 64)
        raw = tokens[span, :].astype(f32)
        average, inverse = row_stats(raw)
        stats[span, :] = jnp.concatenate([average, inverse], axis=1)
        value = (raw - average) * inverse * norm[0:1, :] + norm[1:2, :]
        normed[span, :] = value.astype(bf16)

    each_block(count, 64, normalize)
    weights = weights()
    half = KEY // 2
    cosine, sine = angles[:, :half], angles[:, half:]
    for part in range(2):
        raw = contract(normed[...], weights[:, part * KEY : (part + 1) * KEY], 1, 0)
        turned = turn(raw, cosine, sine)
        qkv[:, part * KEY : (part + 1) * KEY] = (turned * key_scale if part else turned).astype(bf16)
    qkv[:, 2 * KEY :] = contract(normed[...], weights[:, 2 * KEY : QKV], 1, 0).astype(bf16)
    gate[...] = contract(normed[...], weights[:, QKV:], 1, 0)


def decays(columns, rows, away, at, chunk, place, by_query):
    span = slice(at * chunk, (at + 1) * chunk)
    ids, begin = columns[span, 0:1], columns[span, 1:2]
    others, other_begin = rows[0:1, place], rows[1:2, place]
    if by_query:
        mask = (others <= ids) & (others >= begin)
        near = columns[span, 2:3]
    else:
        mask = (others >= ids) & (other_begin <= ids)
        near = columns[span, 3:4]
    return jnp.where(mask, near * away[at : at + 1, place], 0.0)


def spans_of(arrays):
    at = 0
    for array in arrays:
        yield array, slice(at, at + array.shape[0])
        at += array.shape[0]


def branch_body(own, every, gate, columns, rows, away, *refs):
    (own,), (gate,), (columns,), (rows,), (away,) = own, gate, columns, rows, away
    *parts, gated, grouped, inverse, intra, out_weight = refs
    count = own.shape[0]
    chunks = away.shape[0]
    chunk = count // chunks
    queries = own[:, :KEY]
    for array, place in spans_of(every):
        scores = contract(queries, array[:, KEY : 2 * KEY], 1, 1)
        for at in range(chunks):
            factor = decays(columns, rows, away, at, chunk, place, True)
            span = slice(at * chunk, (at + 1) * chunk)
            intra[span, place] = (scores[span] * factor).astype(bf16)
    retained = 0.0
    for array, place in spans_of(every):
        retained = retained + contract(intra[:, place], array[:, 2 * KEY :], 1, 0)
    grouped[...] = retained

    def finish(first):
        span = pl.ds(first, 64)
        value = grouped[span, :]
        average = jnp.mean(value, axis=1, keepdims=True)
        square = jnp.mean(value * value, axis=1, keepdims=True)
        scale = lax.rsqrt(square - average * average + group_epsilon)
        inverse[span, :] = scale
        value = (value - average) * scale
        grouped[span, :] = value
        pre = gate[span, :]
        gated[span, :] = (pre * sigmoid(pre) * value).astype(bf16)

    each_block(count, 64, finish)
    store_parts(parts, count, lambda place, weight=out_weight(): contract(gated[...], weight[:, place], 1, 0))


def store_parts(parts, count, product):
    if parts[0].shape[0] < count:
        value = product(slice(None)).astype(bf16)
        first = 0
        for part in parts:
            part[...] = value[first : first + part.shape[0], :]
            first += part.shape[0]
        return
    first = 0
    for part in parts:
        width = part.shape[1]
        part[...] = product(slice(first, first + width)).astype(bf16)
        first += width


def feed_body(pieces, grad_pieces, rows, grad_rows, active, grad_hidden, *refs):
    *parts, work, up_weight, down_weight = refs
    stage_rows(pieces, rows)
    stage_rows(grad_pieces, grad_rows)
    up_weight = up_weight()
    work[0] = contract(rows[...], up_weight[...], 1, 0)
    work[1] = contract(grad_rows[...], down_weight()[...], 1, 1)

    def finish(first):
        span = pl.ds(first, 32)
        hidden, grad_active = work[0, span, :], work[1, span, :]
        cumulative = 0.5 * (1.0 + lax.erf(hidden * 0.7071067811865476))
        density = jnp.exp(-0.5 * hidden * hidden) * 0.3989422804014327
        active[span, :] = (hidden * cumulative).astype(bf16)
        grad_hidden[span, :] = (grad_active * (cumulative + hidden * density)).astype(bf16)

    each_block(rows.shape[0], 32, finish)
    store_parts(parts, rows.shape[0], lambda place: contract(grad_hidden[...], up_weight[place, :], 1, 1))


def down_body(active, down_weight, *parts):
    (down_weight,) = down_weight
    for value, targets in zip(active, (parts[:3], parts[3:4], parts[4:])):
        store_parts(targets, value.shape[0], lambda place: contract(value[...], down_weight[:, place], 1, 0))


def gate_body(pieces, gate, grouped, inverse, rows, grad_gate, grad_retained, work, out_weight):
    (gate,), (grouped,), (inverse,) = gate, grouped, inverse
    stage_rows(pieces, rows)
    work[...] = contract(rows[...], out_weight()[...], 1, 1)

    def finish(first):
        span = pl.ds(first, 64)
        grad_gated, pre, value = work[span, :], gate[span, :], grouped[span, :]
        sigma = sigmoid(pre)
        grad_gate[span, :] = (grad_gated * value * (sigma * (1.0 + pre * (1.0 - sigma)))).astype(bf16)
        grads = grad_gated * (pre * sigma)
        plain = jnp.mean(grads, axis=1, keepdims=True)
        cross = jnp.mean(grads * value, axis=1, keepdims=True)
        grad_retained[span, :] = (inverse[span, :] * (grads - plain - value * cross)).astype(bf16)

    each_block(rows.shape[0], 64, finish)


def query_body(grads, every, columns, rows, away, angles, split, grad_query, plain_query):
    (grads,), (columns,), (rows,), (away,), (angles,), (split,) = grads, columns, rows, away, angles, split
    chunks = away.shape[0]
    chunk = grads.shape[0] // chunks
    total = 0.0
    for array, place in spans_of(every):
        scores = contract(grads[...], array[:, 2 * KEY :], 1, 1)
        scores = jnp.concatenate(
            [
                (
                    scores[at * chunk : (at + 1) * chunk]
                    * decays(columns, rows, away, at, chunk, place, True)
                ).astype(bf16)
                for at in range(chunks)
            ],
            axis=0,
        )
        total = total + contract(scores, array[:, KEY : 2 * KEY], 1, 0)
    half = KEY // 2
    value = turn(total, angles[:, :half], -angles[:, half:]).astype(bf16)
    grad_query[...] = value
    plain_query[...] = contract(value, split[...], 1, 1).astype(bf16)


def key_body(
    own, every, every_grad, columns, rows, away, angles, split, others, stats,
    grad_key, plain_key, grad_value, sums, *refs,
):
    (own,), (columns,), (rows,), (away,), (angles,), (split,) = own, columns, rows, away, angles, split
    (grad_query, grad_gate), (stats,) = others, stats
    *parts, work, weights, tokens = refs
    chunks = away.shape[0]
    count = own.shape[0]
    chunk = count // chunks
    total_key, total_value = 0.0, 0.0
    for (array, place), grads in zip(spans_of(every), every_grad):
        scores = contract(own[:, KEY : 2 * KEY], array[:, :KEY], 1, 1)
        grad_scores = contract(own[:, 2 * KEY :], grads[...], 1, 1)
        intra, grad_intra = [], []
        for at in range(chunks):
            factor = decays(columns, rows, away, at, chunk, place, False)
            span = slice(at * chunk, (at + 1) * chunk)
            intra.append((scores[span] * factor).astype(bf16))
            grad_intra.append((grad_scores[span] * factor).astype(bf16))
        total_value = total_value + contract(jnp.concatenate(intra, axis=0), grads[...], 1, 0)
        total_key = total_key + contract(jnp.concatenate(grad_intra, axis=0), array[:, :KEY], 1, 0)
    half = KEY // 2
    value = (turn(total_key, angles[:, :half], -angles[:, half:]) * key_scale).astype(bf16)
    grad_key[...] = value
    plain_key[...] = contract(value, split[...], 1, 1).astype(bf16)
    grad_value[...] = total_value.astype(bf16)
    work[:, :KEY] = grad_query[...]
    work[:, KEY : 2 * KEY] = value
    work[:, 2 * KEY : QKV] = grad_value[...]
    work[:, QKV:] = grad_gate[...]
    average, inverse = stats[:, 0:1], stats[:, 1:2]
    weights, tokens = weights(), tokens()
    tile = 512
    by_rows = parts[0].shape[0] < count
    for at in range(0, tokens.shape[1], tile):
        place = slice(at, at + tile)
        value = contract(work[...], weights[place, :], 1, 1)
        first = 0
        for part in parts:
            if by_rows:
                part[:, place] = value[first : first + part.shape[0], :].astype(bf16)
                first += part.shape[0]
            else:
                if first <= at < first + part.shape[1]:
                    part[:, at - first : at - first + tile] = value.astype(bf16)
                first += part.shape[1]
        unit = (tokens[:, place].astype(f32) - average) * inverse
        sums[0:1, place] = jnp.sum(value * unit, axis=0, keepdims=True)
        sums[1:2, place] = jnp.sum(value, axis=0, keepdims=True)


def relay_body(arrived, parts, forth, back, *, halves):
    got_forth, got_back = arrived
    chunk, width = forth.shape[0] // len(parts), forth.shape[1]
    half = width // 2
    for at, part in enumerate(parts):
        span = slice(at * chunk, (at + 1) * chunk)
        if halves:
            forth[span, :half] = (part[chunk:, :half].astype(f32) + got_forth[span, :].astype(f32)).astype(bf16)
            forth[span, half:] = part[chunk:, half:]
            back[span, :half] = part[:chunk, :half]
            back[span, half:] = (part[:chunk, half:].astype(f32) + got_back[span, :].astype(f32)).astype(bf16)
        else:
            forth[span, :] = (part[chunk:, :].astype(f32) + got_forth[span, :].astype(f32)).astype(bf16)
            back[span, :] = (part[:chunk, :].astype(f32) + got_back[span, :].astype(f32)).astype(bf16)


def finish_feed_body(values, up_grad, down_grad):
    total = values[0][...].astype(f32)
    for value in values[1:]:
        total = total + value[...].astype(f32)
    units = up_grad.shape[1]
    up_grad[...] = total[:, :units]
    down_grad[...] = total[:, units:].T


def finish_body(values, *outs):
    first = 0
    for out in outs:
        place = slice(first, first + out.shape[1])
        total = values[0][:, place].astype(f32)
        for value in values[1:]:
            total = total + value[:, place].astype(f32)
        out[...] = total
        first += out.shape[1]


def finish_rows_body(arrived, parts, middle, tokens, stats, gain, layer_out, tokens_grad):
    (middle, grad_middle), (tokens,), (stats,), (gain,) = middle, tokens, stats, gain
    got_forth, got_back = arrived
    count = tokens.shape[0]

    def finish(first):
        span = pl.ds(first, 64)
        totals = []
        for at, part in enumerate(parts):
            here = pl.ds(first + at * count, 64)
            totals.append(
                part[span, :].astype(f32) + got_forth[here, :].astype(f32) + got_back[here, :].astype(f32)
            )
        layer_out[span, :] = middle[span, :] + totals[1]
        inverse = stats[span, 1:2]
        unit = (tokens[span, :].astype(f32) - stats[span, 0:1]) * inverse
        tokens_grad[span, :] = grad_middle[span, :] + normalize_back(totals[0], unit, inverse, gain[0:1, :])

    each_block(count, 64, finish)


def product_shard(wide, groups, ranks, spot, arrived, left_sharded):
    cuts = [group[0].shape[1] // ranks for group in groups]
    width = wide[0].shape[1]
    if any(cut % 128 for cut in cuts):
        columns = [
            jnp.concatenate([lax.dynamic_slice_in_dim(batch, spot * cut, cut, 1) for batch in group], axis=0)
            for group, cut in zip(groups, cuts)
        ]
        columns, wide = jnp.concatenate(columns, axis=1), jnp.concatenate(wide, axis=0)
        total = contract(columns, wide, 0, 0) if left_sharded else contract(wide, columns, 0, 0)
        for value in arrived:
            total = total + value.astype(f32)
        return total.astype(bf16)
    steps = 4
    tile = width // steps
    count, total_cut = len(wide), sum(cuts)

    def kernel(spot_ref, *refs):
        narrow = refs[count : count + count * len(groups)]
        others, out = refs[count + count * len(groups) : -1], refs[-1]
        total = 0.0
        for i in range(count):
            columns = [narrow[g * count + i][...] for g in range(len(groups))]
            columns = columns[0] if len(columns) == 1 else jnp.concatenate(columns, axis=1)
            one = refs[i][...]
            total = total + (contract(columns, one, 0, 0) if left_sharded else contract(one, columns, 0, 0))
        for value in others:
            total = total + value[...].astype(f32)
        out[...] = total.astype(bf16)

    if left_sharded:
        shape, out_spec = (total_cut, width), pl.BlockSpec((total_cut, tile), lambda g, spot_ref: (0, g))
    else:
        shape, out_spec = (width, total_cut), pl.BlockSpec((tile, total_cut), lambda g, spot_ref: (g, 0))
    return pl.pallas_call(
        kernel,
        grid_spec=pltpu.PrefetchScalarGridSpec(
            num_scalar_prefetch=1,
            grid=(steps,),
            in_specs=[pl.BlockSpec((batch.shape[0], tile), lambda g, spot_ref: (0, g)) for batch in wide]
            + [
                pl.BlockSpec((batch.shape[0], cut), lambda g, spot_ref: (0, spot_ref[0]))
                for group, cut in zip(groups, cuts)
                for batch in group
            ]
            + [out_spec] * len(arrived),
            out_specs=out_spec,
        ),
        out_shape=jax.ShapeDtypeStruct(shape, bf16),
        compiler_params=pltpu.CompilerParams(vmem_limit_bytes=24 << 20),
        cost_estimate=pl.CostEstimate(flops=0, transcendentals=0, bytes_accessed=0),
        name="product_shard",
    )(spot.reshape(1).astype(jnp.int32), *wide, *[batch for group in groups for batch in group], *arrived)


def local(
    tokens,
    lengths,
    norm_gains,
    norm_biases,
    w_query,
    w_key,
    w_value,
    w_gate,
    w_out,
    w_up,
    w_down,
    out_grad,
):
    mp_size = lax.axis_size("mp")
    seq_size = lax.axis_size("seq")
    ranks = mp_size // HEADS
    mp_index = lax.axis_index("mp")
    head = mp_index // ranks
    rank = mp_index % ranks
    chunk, width = tokens.shape
    half = width // 2
    own_rows = chunk * HEADS
    sizes = [chunk * len(batch) for batch in BATCHES]

    def ring_shift(value, step):
        pairs = [
            (RING[k] * ranks + r, RING[(k + step) % HEADS] * ranks + r)
            for k in range(HEADS)
            for r in range(ranks)
        ]
        return lax.ppermute(value, "mp", pairs)

    def rank_shift(value, by):
        pairs = [(h * ranks + r, h * ranks + (r + by) % ranks) for h in range(HEADS) for r in range(ranks)]
        return lax.ppermute(value, "mp", pairs)

    def gather_ring(block, work=None, ready=(), hook=None):
        results = []
        hook = hook or (lambda step, pieces: None)

        swaps = []

        def use(at, pieces):
            if work:
                result, sent = work(at, after(pieces, results[-1:], swaps[:at]))
                results.append(result)
                swaps.append(sent if at == 0 else ())

        forth, back = block, block
        near = [block]
        for _ in range(2):
            forth, back = lax.optimization_barrier((ring_shift(forth, 1), ring_shift(back, -1)))
            near += [forth, back]
            hook(len(near) // 2, (forth, back))
        if callable(ready):
            ready = ready(near[1:3])
        forth, back = after((forth, back), ready)
        forth, back = lax.optimization_barrier((ring_shift(forth, 1), ring_shift(back, -1)))
        hook(3, (forth, back))
        use(0, near)
        far = [forth, back]
        left, right = after((forth[:, :half], back[:, half:]), results)
        left, right = ring_shift(left, 1), ring_shift(right, -1)
        use(1, far)
        ends = list(lax.optimization_barrier((left, right)))
        hook(4, ends)
        use(2, ends)
        return [near, far, ends], results

    def stack(values):
        return values[0] if len(values) == 1 else jnp.concatenate(values, axis=0)

    def scatter_ring(*part_of, hook=None):
        count = len(part_of)
        steps, sends = [], []

        def shift(forth, back):
            forth, back = lax.optimization_barrier((forth, back))
            sends.append((forth, back))
            forth, back = lax.optimization_barrier((ring_shift(forth, 1), ring_shift(back, -1)))
            steps.append((forth, back))
            tie = hook(len(steps), sends[-1], steps[-1]) if hook else None
            return after((forth, back), tie) if tie is not None else (forth, back)

        def relay(arrived, parts, halves=False):
            if count == 1 and halves:
                (part,), (forth, back) = parts, arrived
                return (
                    jnp.concatenate(
                        [(part[chunk:, :half].astype(f32) + forth.astype(f32)).astype(bf16), part[chunk:, half:]],
                        axis=1,
                    ),
                    jnp.concatenate(
                        [part[:chunk, :half], (part[:chunk, half:].astype(f32) + back.astype(f32)).astype(bf16)],
                        axis=1,
                    ),
                )
            if count == 1:
                (part,), (forth, back) = parts, arrived
                return (
                    (part[chunk:].astype(f32) + forth.astype(f32)).astype(bf16),
                    (part[:chunk].astype(f32) + back.astype(f32)).astype(bf16),
                )
            shape = ((count * chunk, width), bf16)
            return run(
                functools.partial(relay_body, halves=halves), "relay", [shape, shape], [], arrived, parts, free=True
            )

        far = [part(2, ()) for part in part_of]
        arrived = shift(stack([value[0] for value in far]), stack([value[1] for value in far]))
        parts = [part(1, sends[0])[0] for part in part_of]
        forth, back = relay(arrived, parts, True)
        near = None
        for at in (2, 1):
            arrived = shift(forth, back)
            near = near or [part(0, sends[1]) for part in part_of]
            forth, back = relay(arrived, [pieces[at] for pieces in near])
        return shift(forth, back), [pieces[0] for pieces in near], steps

    def collect(shard):
        return [shard] + [rank_shift(shard, t) for t in range(1, ranks)]

    def assemble(pieces, axis):
        ordered = []
        for spot in range(ranks):
            value = pieces[0]
            for t in range(1, ranks):
                value = jnp.where((rank - t + ranks) % ranks == spot, pieces[t], value)
            ordered.append(value)
        return jnp.concatenate(ordered, axis=axis)

    def batch_of(array, at, axis=0):
        first = FIRST[at] * chunk
        return lax.slice_in_dim(array, first, first + sizes[at], axis=axis)

    with jax.named_scope("head_weights"):
        split = np.zeros((KEY, KEY), np.float32)
        for i in range(KEY // 2):
            split[2 * i, i] = 1.0
            split[2 * i + 1, KEY // 2 + i] = 1.0
        split = jnp.asarray(split, bf16)

        def separate(weight):
            return jnp.dot(weight, split, preferred_element_type=f32).astype(bf16)

        query_pieces, key_pieces = collect(w_query), collect(w_key)
        value_pieces = collect(after(w_value, query_pieces[1:]))
        gate_pieces = collect(after(w_gate, key_pieces[1:]))
        in_weights = jnp.concatenate(
            [
                separate(assemble(query_pieces, 1)),
                separate(assemble(key_pieces, 1)),
                assemble(value_pieces, 1),
                assemble(gate_pieces, 1),
            ],
            axis=1,
        )
        out_weight = assemble(collect(after(w_out, value_pieces[1:])), 0)

    with jax.named_scope("row_places"):
        table = np.zeros((HEADS, HEADS), np.int32)
        for k, h in enumerate(RING):
            for j, offset in enumerate(OFFSETS):
                table[h, j] = RING[(k + offset) % HEADS]
        sources = lax.dynamic_slice_in_dim(jnp.asarray(table), head, 1, 0)[0]
        inner = jnp.arange(chunk, dtype=jnp.int32)
        row_ids = jnp.concatenate(
            [
                (((sources * ranks + (rank - t + ranks) % ranks) * chunk)[:, None] + inner[None, :]).reshape(-1)
                for t in range(ranks)
            ]
        )
        ends = jnp.cumsum(lengths[0], dtype=jnp.int32)
        starts = ends - lengths[0]
        member = (row_ids[:, None] >= starts[None, :]) & (row_ids[:, None] < ends[None, :])
        begins = jnp.sum(jnp.where(member, starts[None, :], 0), axis=1, dtype=jnp.int32)
        position = (row_ids - begins)[:own_rows]
        frequencies = 10000.0 ** (-jnp.arange(KEY // 2).astype(f32) / (KEY // 2))
        angles = position.astype(f32)[:, None] * frequencies[None, :]
        angles = jnp.concatenate([jnp.cos(angles), jnp.sin(angles)], axis=1)
        log_decay = jnp.log(1.0 - 2.0 ** (-5.0 - head.astype(f32)))
        bases = row_ids[:own_rows:chunk]

    def away_of(array, at):
        return array[FIRST[at] : FIRST[at] + len(BATCHES[at])]

    normed_rows, own_qkv, gate_pre, stats_one = [None] * 3, [None] * 3, [None] * 3, [None] * 3
    token_rows = [None] * 3
    norm = jnp.stack([norm_gains[0], norm_biases[0]])

    placed = {}

    def ready(first):
        with jax.named_scope("row_factors"):
            ids, begin = row_ids, begins
            away = bases[:, None] - ids[None, :]
            away_query = jnp.exp(jnp.maximum(away, 1 - chunk).astype(f32) * log_decay)
            away_key = jnp.exp(jnp.maximum(-away, 0).astype(f32) * log_decay)
            near = jnp.tile(inner.astype(f32) * log_decay, HEADS)
            columns = jnp.stack(
                [ids[:own_rows].astype(f32), begin[:own_rows].astype(f32), jnp.exp(near), jnp.exp(-near)],
                axis=1,
            )
            values = (
                [batch_of(angles, at) for at in range(3)],
                [batch_of(columns, at) for at in range(3)],
                [away_of(away_query, at) for at in range(3)],
                [away_of(away_key, at) for at in range(3)],
                jnp.stack([ids.astype(f32), begin.astype(f32)]),
                in_weights,
                norm,
            )
            names = ("angles", "columns", "away", "away_key", "rows", "weights", "norm")
            placed.update(zip(names, lax.optimization_barrier(values)))
        return tuple(placed.values())

    def project(at, pieces):
        token_rows[at], normed_rows[at], own_qkv[at], gate_pre[at], stats_one[at] = run(
            project_body,
            "project",
            [
                ((sizes[at], width), bf16),
                ((sizes[at], width), bf16),
                ((sizes[at], QKV), bf16),
                ((sizes[at], VAL), f32),
                ((sizes[at], 2), f32),
            ],
            [],
            pieces,
            placed["norm"],
            placed["angles"][at],
            late=[placed["weights"]],
            flops=2 * sizes[at] * width * (QKV + VAL),
        )
        other_qkv[at] = [rank_shift(own_qkv[at], t) for t in range(1, ranks)]
        return (own_qkv[at], out_weight) if at == 0 else own_qkv[at], other_qkv[at]

    other_qkv = [None] * 3
    with jax.named_scope("project_in"):
        token_pieces, _ = gather_ring(tokens, project, ready)
        every_qkv = own_qkv + [other_qkv[at][t] for t in range(ranks - 1) for at in range(3)]
    with jax.named_scope("gather_out_grad"):
        grad_steps = {}
        grad_pieces, _ = gather_ring(after(out_grad, token_pieces[2]), hook=grad_steps.__setitem__)
    with jax.named_scope("feed_weights"):
        up_weight = assemble(collect(after(w_up, token_pieces[2])), 1)
        down_weight = assemble(collect(after(w_down, token_pieces[2])), 0)

    grouped, inverse_group, gated_rows = [None] * 3, [None] * 3, [None] * 3

    def part_shapes(at):
        if at == 0:
            return [((size, width), bf16) for size in (chunk, 2 * chunk, 2 * chunk)]
        return [((sizes[at], half), bf16)] * 2 if at == 2 else [((sizes[at], width), bf16)]

    def branch_part(at, earlier):
        *part, gated_rows[at], grouped[at], inverse_group[at] = run(
            branch_body,
            "branch",
            part_shapes(at)
            + [
                ((sizes[at], VAL), bf16),
                ((sizes[at], VAL), f32),
                ((sizes[at], 1), f32),
            ],
            [((sizes[at], ranks * own_rows), bf16)],
            after(own_qkv[at], earlier, grad_steps[1] if at == 0 else ()),
            every_qkv,
            gate_pre[at],
            placed["columns"][at],
            placed["rows"],
            placed["away"][at],
            late=[out_weight],
            flops=2 * sizes[at] * (ranks * own_rows * (KEY + VAL) + VAL * width),
        )
        return part

    with jax.named_scope("retention"):
        (forth, back), (part,), _ = scatter_ring(branch_part)
        middle = tokens.astype(f32) + (part.astype(f32) + forth.astype(f32) + back.astype(f32))

    def shard(left, right, left_sharded, spot):
        cuts = left if left_sharded else right
        cut = cuts.shape[1] // ranks
        piece = lax.dynamic_slice_in_dim(cuts, spot * cut, cut, 1)
        return contract(piece, right, 0, 0) if left_sharded else contract(left, piece, 0, 0)

    def send_shards(left, right, left_sharded):
        others = [shard(left, right, left_sharded, (rank + t) % ranks).astype(bf16) for t in range(1, ranks)]
        return others, [rank_shift(value, t + 1) for t, value in enumerate(others)]

    def own_shard(left, right, left_sharded, arrived):
        result = shard(left, right, left_sharded, rank)
        for value in arrived:
            result = result + value.astype(f32)
        return result.astype(bf16)

    def send_groups(value):
        return [
            lax.ppermute(value, "seq", [(i, (i + t) % seq_size) for i in range(seq_size)])
            for t in range(1, seq_size)
        ]

    def finish(value, arrived, widths, *late):
        outs = [((value.shape[0], size), f32) for size in widths]
        return run(finish_body, "finish", outs, [], [value, *after(arrived, *late)], free=True)

    def joined(batches):
        return jnp.concatenate(batches, axis=0)

    def by_rank(*values):
        cuts = [value.shape[1] // ranks for value in values]
        return jnp.concatenate(
            [value[:, r * cut : (r + 1) * cut] for r in range(ranks) for value, cut in zip(values, cuts)], axis=1
        )

    with jax.named_scope("norm_two"):
        average, inverse_two = row_stats(middle)
        unit_two = (middle - average) * inverse_two
        normed_two = (unit_two * norm_gains[1] + norm_biases[1]).astype(bf16)
    up_parts, two_rows, grad_rows = [None] * 3, [None] * 3, [None] * 3
    active_rows, grad_hidden_rows = [None] * 3, [None] * 3

    def feed(at, pieces):
        two_rows[at], grad_rows[at], active_rows[at], grad_hidden_rows[at], *up_parts[at] = run(
            feed_body,
            "feed",
            [
                ((sizes[at], width), bf16),
                ((sizes[at], width), bf16),
                ((sizes[at], VAL), bf16),
                ((sizes[at], VAL), bf16),
            ]
            + part_shapes(at),
            [((2, sizes[at], VAL), f32)],
            pieces,
            grad_pieces[at],
            late=[up_weight, down_weight],
            flops=6 * sizes[at] * width * VAL,
        )
        return active_rows[at], ()

    with jax.named_scope("feed_forward"):
        gather_ring(normed_two, feed)
    early = {}

    def up_hook(step, sends, arrived):
        if step == 1:
            with jax.named_scope("down_grad"):
                left, right = joined(after(grad_rows, sends)), joined(after(active_rows, sends))
                others, got = send_shards(left, right, False)
                early["down"] = own_shard(left, right, False, got)
        if step == 2:
            with jax.named_scope("up_grad"):
                left, right = joined(after(two_rows, sends)), joined(after(grad_hidden_rows, sends))
                others, got = send_shards(left, right, False)
                early["up"] = jnp.concatenate(
                    [own_shard(left, right, False, got), early["down"]], axis=1
                )
        if step == 3:
            with jax.named_scope("down_parts"):
                parts = run(
                    down_body,
                    "down",
                    part_shapes(0) + part_shapes(1) + part_shapes(2),
                    [],
                    after(active_rows, sends),
                    down_weight,
                    flops=2 * own_rows * width * VAL,
                )
                early["parts"] = [parts[:3], parts[3:4], parts[4:]]

    with jax.named_scope("scatter_up"):
        (forth, back), (part,), up_steps = scatter_ring(lambda at, earlier: up_parts[at], hook=up_hook)
        grad_normed_two = part.astype(f32) + forth.astype(f32) + back.astype(f32)
    feed_own, down_parts = early["up"], early["parts"]
    with jax.named_scope("norm_two_back"):
        grad_middle = out_grad.astype(f32) + normalize_back(
            grad_normed_two, unit_two, inverse_two, norm_gains[1]
        )
        grad_branch = grad_middle.astype(bf16)
        gain_two = jnp.sum(grad_normed_two * unit_two, axis=0)
        bias_two = jnp.sum(grad_normed_two, axis=0)

    branch_rows, grad_gate, own_grad = [None] * 3, [None] * 3, [None] * 3
    grad_query, plain_query = [None] * 3, [None] * 3

    def gate_back(at, pieces):
        branch_rows[at], grad_gate[at], own_grad[at] = run(
            gate_body,
            "gate_back",
            [
                ((sizes[at], width), bf16),
                ((sizes[at], VAL), bf16),
                ((sizes[at], VAL), bf16),
            ],
            [((sizes[at], VAL), f32)],
            pieces,
            gate_pre[at],
            grouped[at],
            inverse_group[at],
            late=[out_weight],
            flops=2 * sizes[at] * width * VAL,
        )
        other_grad[at] = [rank_shift(own_grad[at], t) for t in range(1, ranks)]
        return own_grad[at], other_grad[at]

    other_grad = [None] * 3
    with jax.named_scope("gate_back"):
        branch_pieces, _ = gather_ring(after(grad_branch, feed_own, down_parts), gate_back)
        every_grad = own_grad + [other_grad[at][t] for t in range(ranks - 1) for at in range(3)]
    with jax.named_scope("feed_grads"):
        feed_got = send_groups(feed_own)

    def query_back(at, earlier):
        with jax.named_scope("query_back"):
            grad_query[at], plain_query[at] = run(
                query_body,
                "query_back",
                [((sizes[at], KEY), bf16)] * 2,
                [],
                after(own_grad[at], earlier),
                every_qkv,
                placed["columns"][at],
                placed["rows"],
                placed["away"][at],
                placed["angles"][at],
                split,
                free=True,
            )

    def other_shards(wide, groups, left_sharded):
        others = [
            product_shard(wide, groups, ranks, (rank + t) % ranks, (), left_sharded) for t in range(1, ranks)
        ]
        return others, [rank_shift(value, t + 1) for t, value in enumerate(others)]

    with jax.named_scope("out_grad"):
        out_others, out_got = other_shards(branch_rows, [gated_rows], True)
    late_own = {}
    grad_value, plain_key = [None] * 3, [None] * 3
    norm_sums = []
    out_exchange, gate_exchange, last_exchange = [], [], {}

    def in_part(at, earlier):
        query_back(at, earlier or out_others)
        if at == 2:
            earlier = feed_got
        if at == 1:
            with jax.named_scope("out_grad"):
                wide = after(branch_rows, earlier)
                late_own["out"] = product_shard(wide, [gated_rows], ranks, rank, out_got, True)
                out_exchange.extend(send_groups(late_own["out"]))
            with jax.named_scope("gate_grad"):
                _, late_own["got"] = other_shards(after(normed_rows, earlier), [grad_gate], False)
        if at == 0:
            with jax.named_scope("gate_grad"):
                wide = after(normed_rows, earlier)
                late_own["gate"] = product_shard(wide, [grad_gate], ranks, rank, late_own["got"], False)
        _, plain_key[at], grad_value[at], sums, *part = run(
            key_body,
            "key_back",
            [
                ((sizes[at], KEY), bf16),
                ((sizes[at], KEY), bf16),
                ((sizes[at], VAL), bf16),
                ((2, width), f32),
            ]
            + part_shapes(at),
            [((sizes[at], QKV + VAL), bf16)],
            after(own_qkv[at], earlier, late_own["gate"] if at == 0 else ()),
            every_qkv,
            every_grad,
            placed["columns"][at],
            placed["rows"],
            placed["away_key"][at],
            placed["angles"][at],
            split,
            [grad_query[at], grad_gate[at]],
            stats_one[at],
            late=[placed["weights"], token_rows[at]],
            free=True,
        )
        norm_sums.append(sums)
        return part

    finished = {}

    def finish_early(late):
        units = w_up.shape[1]
        with jax.named_scope("feed_grads"):
            feed_late = after(feed_got, late)
            if units % 128:
                both = sum(value.astype(f32) for value in (feed_own, *feed_late))
                finished["up"], finished["down"] = both[:, :units], both[:, units:].T
            else:
                shapes = [((width, units), f32), ((units, width), f32)]
                finished["up"], finished["down"] = run(
                    finish_feed_body, "finish_feed", shapes, [], [feed_own, *feed_late], free=True
                )
        with jax.named_scope("out_grad"):
            (finished["out"],) = finish(late_own["out"], out_exchange, [width], late)
        return tuple(finished.values())

    with jax.named_scope("key_back"):
        def in_hook(step, sends, arrived):
            if step == 2:
                return out_exchange
            if step == 4:
                with jax.named_scope("gate_grad"):
                    (finished["gate"],) = finish(late_own["gate"], gate_exchange, [VAL // ranks], sends)
                return None
            if step != 3:
                return None
            late_own["sends"] = sends
            gate_exchange.extend(send_groups(late_own["gate"]))
            for name, groups in (("value", [grad_value]), ("query_key", [plain_query, plain_key])):
                with jax.named_scope(name + "_grad"):
                    wide = after(normed_rows, sends)
                    _, got = other_shards(wide, groups, False)
                    if name == "query_key":
                        wide = after(wide, finish_early(late_own["value"]), gate_exchange)
                    late_own[name] = product_shard(wide, groups, ranks, rank, got, False)
                    last_exchange[name] = send_groups(late_own[name])
            return late_own["value"]

        arrived, parts, in_steps = scatter_ring(in_part, lambda at, earlier: down_parts[at], hook=in_hook)
    with jax.named_scope("finish_rows"):
        layer_out, tokens_grad = run(
            finish_rows_body,
            "finish_rows",
            [((chunk, width), f32)] * 2,
            [],
            after(arrived, last_exchange["value"]),
            parts,
            [middle, grad_middle],
            tokens,
            stats_one[0][:chunk],
            placed["norm"],
            free=True,
        )

    def sum_groups(value):
        result = value
        for t in range(1, seq_size):
            pairs = [(i, (i + t) % seq_size) for i in range(seq_size)]
            result = result + lax.ppermute(value, "seq", pairs)
        return result

    with jax.named_scope("norm_grads"):
        gain_one, bias_one = sum(norm_sums)
        total = after(jnp.stack([gain_one, gain_two, bias_one, bias_two]), in_steps[3])

        def from_others(values, across):
            result = values
            for bits in across:
                pairs = [(h * ranks + r, (h ^ bits) * ranks + r) for h in range(HEADS) for r in range(ranks)]
                result = result + lax.ppermute(values, "mp", pairs)
            return result

        shared = total
        for t in range(1, ranks):
            shared = shared + rank_shift(total, t)
        total = from_others(after(shared, tokens_grad), (1, 2, 3))
        with jax.named_scope("value_grad"):
            (value_grad,) = finish(late_own["value"], last_exchange["value"], [VAL // ranks], tokens_grad)
        total = from_others(after(total, value_grad), (4,))
        span = width // mp_size
        mine = sum_groups(lax.dynamic_slice_in_dim(total, mp_index * span, span, 1))

    with jax.named_scope("query_key_grad"):
        query_grad, key_grad = finish(
            late_own["query_key"], last_exchange["query_key"], [KEY // ranks] * 2, value_grad, finished["gate"]
        )
    return (
        layer_out,
        tokens_grad,
        query_grad,
        key_grad,
        value_grad,
        finished["gate"],
        finished["out"],
        finished["up"],
        finished["down"],
        mine[:2],
        mine[2:],
    )


def solution(mesh):
    return jax.shard_map(
        local,
        mesh=mesh,
        in_specs=(
            P(("seq", "mp"), None),
            P("seq", None),
            P(),
            P(),
            P(None, "mp"),
            P(None, "mp"),
            P(None, "mp"),
            P(None, "mp"),
            P("mp", None),
            P(None, "mp"),
            P("mp", None),
            P(("seq", "mp"), None),
        ),
        out_specs=(
            P(("seq", "mp"), None),
            P(("seq", "mp"), None),
            P(None, "mp"),
            P(None, "mp"),
            P(None, "mp"),
            P(None, "mp"),
            P("mp", None),
            P(None, "mp"),
            P("mp", None),
            P(None, "mp"),
            P(None, "mp"),
        ),
        check_vma=False,
    )
```

profile of v0, /device:TPU:0, one launch (start us, length us, event | category | flops | bytes accessed | tf_op | source)
XLA Modules:
  0.0 422.0 jit_solution(5880750722220764421)
XLA Ops:
  0.7 3.0 collective-permute-start.1
  9.6 1.9 multiply_sine_fusion
  23.9 5.9 %collective-permute-done.2.refs_3_ = bf16[128,2048]{1,0:T(8,128)(2,1)S(1)} collective-permute-done((bf16[128,2048]{1,0:T(8,128)(2,1)S(1)}, bf16[128,2048]{1,0:T(8,128)(2,1)S(1)}, u32[]{:S(2)}, u32[]{:S(2)}) %collective-permute-start.2) | collective-permute-done | bytes 524320 | tf_op jit(solution)/shard_map/project_in/ppermute | solution.py:492
  31.8 1.6 collective-permute-start.8
  33.9 7.7 %project.3 = (bf16[640,2048]{1,0:T(8,128)(2,1)S(1)}, bf16[640,2048]{1,0:T(8,128)(2,1)S(1)}, bf16[640,1024]{1,0:T(8,128)(2,1)S(1)}, f32[640,512]{1,0:T(8,128)S(1)}, f32[640,2]{1,0:T(8,128)S(1)}) custom-call(bf16[128,2048]{1,0:T(8,128)(2,1)S(1)} %copy-done.44, bf16[128,2048]{1,0:T(8,128)(2,1)S(1)} %collective-permute-done.refs_1_, ...), custom_call_target="tpu_custom_call" | custom-call | flops 4026531840 | bytes 17454080 | tf_op jit(solution)/shard_map/project_in/project/pallas_call | solution.py:101
  41.8 4.4 %collective-permute-done.8.refs_0_ = bf16[128,2048]{1,0:T(8,128)(2,1)S(1)} collective-permute-done((bf16[128,2048]{1,0:T(8,128)(2,1)S(1)}, bf16[128,2048]{1,0:T(8,128)(2,1)S(1)}, u32[]{:S(2)}, u32[]{:S(2)}) %collective-permute-start.8) | collective-permute-done | bytes 524320 | tf_op jit(solution)/shard_map/project_in/ppermute | solution.py:492
  50.2 3.5 project.4
  53.9 1.7 collective-permute-done.11.refs_0_
  57.1 2.1 project.5
  61.5 1.7 branch.3
  65.4 2.8 branch.4
  68.3 11.2 %collective-permute-done.16 = bf16[128,1024]{1,0:T(8,128)(2,1)S(1)} collective-permute-done((bf16[128,1024]{1,0:T(8,128)(2,1)S(1)}, bf16[128,1024]{1,0:T(8,128)(2,1)S(1)}, u32[]{:S(2)}, u32[]{:S(2)}) %collective-permute-start.16) | collective-permute-done | bytes 262176 | tf_op jit(solution)/shard_map/retention/ppermute | solution.py:492
  79.7 1.6 collective-permute-start.20
  81.9 6.0 %branch.5 = (bf16[128,2048]{1,0:T(8,128)(2,1)S(1)}, bf16[256,2048]{1,0:T(8,128)(2,1)S(1)}, bf16[256,2048]{1,0:T(8,128)(2,1)S(1)}, bf16[640,512]{1,0:T(8,128)(2,1...) custom-call(bf16[640,1024]{1,0:T(8,128)(2,1)S(1)} %get-tuple-element.533.refs_1_.refs_0_, ...), custom_call_target="tpu_custom_call" | custom-call | flops 3355443200 | bytes 13570560 | tf_op jit(solution)/shard_map/retention/branch/pallas_call | solution.py:101
  89.9 3.2 collective-permute-done.20
  99.2 10.4 %collective-permute-done.22 = bf16[128,2048]{1,0:T(8,128)(2,1)S(1)} collective-permute-done((bf16[128,2048]{1,0:T(8,128)(2,1)S(1)}, bf16[128,2048]{1,0:T(8,128)(2,1)S(1)}, u32[]{:S(2)}, u32[]{:S(2)}) %collective-permute-start.22) | collective-permute-done | bytes 524320 | tf_op jit(solution)/shard_map/retention/ppermute | solution.py:492
  114.5 6.5 %collective-permute-done.30.refs_8_ = bf16[128,2048]{1,0:T(8,128)(2,1)} collective-permute-done((bf16[128,2048]{1,0:T(8,128)(2,1)}, bf16[128,2048]{1,0:T(8,128)(2,1)}, u32[]{:S(2)}, u32[]{:S(2)}) %collective-permute-start.30) | collective-permute-done | bytes 524320 | tf_op jit(solution)/shard_map/gather_out_grad/ppermute | solution.py:492
  123.4 8.8 %collective-permute-done.24 = bf16[128,2048]{1,0:T(8,128)(2,1)} collective-permute-done((bf16[128,2048]{1,0:T(8,128)(2,1)}, bf16[128,2048]{1,0:T(8,128)(2,1)}, u32[]{:S(2)}, u32[]{:S(2)}) %collective-permute-start.24) | collective-permute-done | bytes 524320 | tf_op jit(solution)/shard_map/retention/ppermute | solution.py:492
  132.7 2.0 fusion.48
  137.7 15.3 %collective-permute-done.27.refs_2_ = bf16[128,2048]{1,0:T(8,128)(2,1)S(1)} collective-permute-done((bf16[128,2048]{1,0:T(8,128)(2,1)S(1)}, bf16[128,2048]{1,0:T(8,128)(2,1)S(1)}, u32[]{:S(2)}, u32[]{:S(2)}) %collective-permute-start.27) | collective-permute-done | bytes 524320 | tf_op jit(solution)/shard_map/feed_forward/ppermute | solution.py:492
  157.3 10.5 %collective-permute-done.28.refs_3_ = bf16[128,2048]{1,0:T(8,128)(2,1)S(1)} collective-permute-done((bf16[128,2048]{1,0:T(8,128)(2,1)S(1)}, bf16[128,2048]{1,0:T(8,128)(2,1)S(1)}, u32[]{:S(2)}, u32[]{:S(2)}) %collective-permute-start.28) | collective-permute-done | bytes 524320 | tf_op jit(solution)/shard_map/feed_forward/ppermute | solution.py:492
  171.1 2.4 collective-permute-done.40.refs_2_
  174.4 7.7 %feed.3 = (bf16[640,2048]{1,0:T(8,128)(2,1)S(1)}, bf16[640,2048]{1,0:T(8,128)(2,1)S(1)}, bf16[640,512]{1,0:T(8,128)(2,1)S(1)}, bf16[640,512]{1,0:T(8,128)(2,1)S(...) custom-call(bf16[128,2048]{1,0:T(8,128)(2,1)S(1)} %add_convert_fusion.6.refs_0_, ...), custom_call_target="tpu_custom_call" | custom-call | flops 4026531840 | bytes 18612224 | tf_op jit(solution)/shard_map/feed_forward/feed/pallas_call | solution.py:101
  184.3 3.0 feed.4
  189.4 2.6 feed.5
  196.3 2.2 collective-permute-done.42
  203.6 7.5 %collective-permute-done.47 = bf16[128,2048]{1,0:T(8,128)(2,1)S(1)} collective-permute-done((bf16[128,2048]{1,0:T(8,128)(2,1)S(1)}, bf16[128,2048]{1,0:T(8,128)(2,1)S(1)}, u32[]{:S(2)}, u32[]{:S(2)}) %collective-permute-start.47) | collective-permute-done | bytes 524320 | tf_op jit(solution)/shard_map/scatter_up/ppermute | solution.py:492
  214.0 2.3 down.1
  218.2 5.4 %collective-permute-done.49 = bf16[128,2048]{1,0:T(8,128)(2,1)S(1)} collective-permute-done((bf16[128,2048]{1,0:T(8,128)(2,1)S(1)}, bf16[128,2048]{1,0:T(8,128)(2,1)S(1)}, u32[]{:S(2)}, u32[]{:S(2)}) %collective-permute-start.49) | collective-permute-done | bytes 524320 | tf_op jit(solution)/shard_map/scatter_up/ppermute | solution.py:492
  228.0 5.6 %collective-permute-done.51 = bf16[128,2048]{1,0:T(8,128)(2,1)S(1)} collective-permute-done((bf16[128,2048]{1,0:T(8,128)(2,1)S(1)}, bf16[128,2048]{1,0:T(8,128)(2,1)S(1)}, u32[]{:S(2)}, u32[]{:S(2)}) %collective-permute-start.51) | collective-permute-done | bytes 524320 | tf_op jit(solution)/shard_map/scatter_up/ppermute | solution.py:492
  240.8 9.3 %collective-permute-done.54.refs_2_ = bf16[128,2048]{1,0:T(8,128)(2,1)S(1)} collective-permute-done((bf16[128,2048]{1,0:T(8,128)(2,1)S(1)}, bf16[128,2048]{1,0:T(8,128)(2,1)S(1)}, u32[]{:S(2)}, u32[]{:S(2)}) %collective-permute-start.54) | collective-permute-done | bytes 524320 | tf_op jit(solution)/shard_map/gate_back/ppermute | solution.py:492
  250.1 3.5 collective-permute-done.53.refs_1_
  254.0 1.7 collective-permute-start.56
  255.7 12.0 %collective-permute-done.55.refs_3_ = bf16[128,2048]{1,0:T(8,128)(2,1)S(1)} collective-permute-done((bf16[128,2048]{1,0:T(8,128)(2,1)S(1)}, bf16[128,2048]{1,0:T(8,128)(2,1)S(1)}, u32[]{:S(2)}, u32[]{:S(2)}) %collective-permute-start.55) | collective-permute-done | bytes 524320 | tf_op jit(solution)/shard_map/gate_back/ppermute | solution.py:492
  270.3 3.9 gate_back.3
  274.4 2.9 collective-permute-done.57.refs_0_
  278.6 1.8 collective-permute-start.60
  280.7 1.8 gate_back.4
  282.4 2.6 collective-permute-done.60.refs_0_
  285.0 1.7 collective-permute-done.61.refs_1_
  288.3 2.7 product_shard.8
  294.3 4.8 %key_back.3 = (bf16[128,256]{1,0:T(8,128)(2,1)}, bf16[128,256]{1,0:T(8,128)(2,1)S(1)}, bf16[128,512]{1,0:T(8,128)(2,1)S(1)}, f32[2,2048]{1,0:T(2,128)S(1)}, bf16...) custom-call(bf16[128,1024]{1,0:T(8,128)(2,1)S(1)} %get-tuple-element.436.refs_0_.refs_3_, ...), custom_call_target="tpu_custom_call" | custom-call | tf_op jit(solution)/shard_map/key_back/key_back/pallas_call | solution.py:101
  301.8 2.7 product_shard.10
  306.3 5.1 %key_back.4 = (bf16[256,256]{1,0:T(8,128)(2,1)}, bf16[256,256]{1,0:T(8,128)(2,1)S(1)}, bf16[256,512]{1,0:T(8,128)(2,1)S(1)}, f32[2,2048]{1,0:T(2,128)S(1)}, bf16[256,2048]{1,0:T(8,128)(2,1)S(1)}) custom-call(bf16[256,1024]{1,0:T(8,128)(2,1)S(1)} %get-tuple-element.507.refs_2_.refs_0_, bf16[640,1024]{1,0:T(8,128)(2,1)S(1)} %get-tuple-element.533.refs_1_.refs_0_, ...), custom_call_target="tpu_custom_call" | custom-call | tf_op jit(solution)/shard_map/key_back/key_back/pallas_call | solution.py:101
  311.4 1.9 collective-permute-done.64.refs_0_
  313.3 1.6 collective-permute-done.65.refs_1_
  318.1 2.7 product_shard.9.refs_0_
  320.9 1.8 collective-permute-start.69
  322.7 3.4 query_back.5
  326.2 2.7 product_shard.11.refs_0_
  330.4 10.9 %key_back.5 = (bf16[640,256]{1,0:T(8,128)(2,1)}, bf16[640,256]{1,0:T(8,128)(2,1)S(1)}, bf16[640,512]{1,0:T(8,128)(2,1)S(1)}, f32[2,2048]{1,0:T(2,128)S(1)}, bf16...) custom-call(bf16[640,1024]{1,0:T(8,128)(2,1)S(1)} %get-tuple-element.533.refs_1_.refs_0_, ...), custom_call_target="tpu_custom_call" | custom-call | tf_op jit(solution)/shard_map/key_back/key_back/pallas_call | solution.py:101
  341.3 3.1 collective-permute-done.69.refs_1_
  345.0 2.7 product_shard.12
  349.9 1.7 collective-permute-start.77
  351.6 2.8 product_shard.14
  354.5 2.7 product_shard.13.refs_0_
  357.7 15.7 %collective-permute-done.71.refs_0_ = bf16[256,2048]{1,0:T(8,128)(2,1)S(1)} collective-permute-done((bf16[256,2048]{1,0:T(8,128)(2,1)S(1)}, bf16[256,2048]{1,0:T(8,128)(2,1)S(1)}, u32[]{:S(2)}, u32[]{:S(2)}) %collective-permute-start.71) | collective-permute-done | bytes 1048608 | tf_op jit(solution)/shard_map/key_back/ppermute | solution.py:492
  378.2 2.7 finish_feed.1
  381.0 2.9 product_shard.15.refs_0_
  385.4 13.4 %collective-permute-done.74.refs_0_ = bf16[256,2048]{1,0:T(8,128)(2,1)S(1)} collective-permute-done((bf16[256,2048]{1,0:T(8,128)(2,1)S(1)}, bf16[256,2048]{1,0:T(8,128)(2,1)S(1)}, u32[]{:S(2)}, u32[]{:S(2)}) %collective-permute-start.74) | collective-permute-done | bytes 1048608 | tf_op jit(solution)/shard_map/key_back/ppermute | solution.py:492
  399.8 2.2 finish_rows.1
  402.0 1.8 collective-permute-start.83
  409.8 3.6 collective-permute-done.84
  417.7 2.1 collective-permute-done.79.refs_1_
  (513 shorter events, 128.9 us)
Async XLA Ops:
  0.7 15.2 %collective-permute-start.1 = (bf16[128,2048]{1,0:T(8,128)(2,1)}, bf16[128,2048]{1,0:T(8,128)(2,1)S(1)}, u32[]{:S(2)}, u32[]{:S(2)}) collective-permute-start(bf16[128,2048]{1,0:T(8,128)(2,1)} %refs_6_.1), channel_id=1, source_target_pairs={{0,2},{1,3},{4,0},{5,1},{8,4},{9,5},{12,8},{13,9},{14,12},{15,13},... | collective-permute-start | bytes 1572872 | tf_op jit(solution)/shard_map/project_in/ppermute | solution.py:492
  3.7 13.6 %collective-permute-start = (bf16[128,2048]{1,0:T(8,128)(2,1)}, bf16[128,2048]{1,0:T(8,128)(2,1)S(1)}, u32[]{:S(2)}, u32[]{:S(2)}) collective-permute-start(bf16[128,2048]{1,0:T(8,128)(2,1)} %refs_6_.1), channel_id=1, source_target_pairs={{0,4},{1,5},{4,8},{5,9},{8,12},{9,13},{12,14},{13,15},{14,10},{15,... | collective-permute-start | bytes 1572872 | tf_op jit(solution)/shard_map/project_in/ppermute | solution.py:492
  3.8 11.2 %collective-permute-start.4 = (bf16[2048,128]{1,0:T(8,128)(2,1)}, bf16[2048,128]{1,0:T(8,128)(2,1)}, u32[]{:S(2)}, u32[]{:S(2)}) collective-permute-start(bf16[2048,128]{1,0:T(8,128)(2,1)} %param.18), channel_id=1, source_target_pairs={{0,1},{1,0},{2,3},{3,2},{4,5},{5,4},{6,7},{7,6},{8,9},{9,8},{10,11... | collective-permute-start | bytes 1572872 | tf_op jit(solution)/shard_map/head_weights/ppermute | solution.py:496
  3.8 11.2 %collective-permute-start.5 = (bf16[2048,128]{1,0:T(8,128)(2,1)}, bf16[2048,128]{1,0:T(8,128)(2,1)}, u32[]{:S(2)}, u32[]{:S(2)}) collective-permute-start(bf16[2048,128]{1,0:T(8,128)(2,1)} %param.19), channel_id=1, source_target_pairs={{0,1},{1,0},{2,3},{3,2},{4,5},{5,4},{6,7},{7,6},{8,9},{9,8},{10,11... | collective-permute-start | bytes 1572872 | tf_op jit(solution)/shard_map/head_weights/ppermute | solution.py:496
  17.3 12.5 %collective-permute-start.2 = (bf16[128,2048]{1,0:T(8,128)(2,1)S(1)}, bf16[128,2048]{1,0:T(8,128)(2,1)S(1)}, u32[]{:S(2)}, u32[]{:S(2)}) collective-permute-start(bf16[128,2048]{1,0:T(8,128)(2,1)S(1)} %collective-permute-done.refs_1_), channel_id=1, source_target_pairs={{0,4},{1,5},{4,8},{5,9},{8,12},{9,13},{12,14},{13,15},{14,10},{15,... | collective-permute-start | bytes 1572872 | tf_op jit(solution)/shard_map/project_in/ppermute | solution.py:492
  17.7 12.9 %collective-permute-start.3 = (bf16[128,2048]{1,0:T(8,128)(2,1)S(1)}, bf16[128,2048]{1,0:T(8,128)(2,1)S(1)}, u32[]{:S(2)}, u32[]{:S(2)}) collective-permute-start(bf16[128,2048]{1,0:T(8,128)(2,1)S(1)} %collective-permute-done.1.refs_2_), channel_id=1, source_target_pairs={{0,2},{1,3},{4,0},{5,1},{8,4},{9,5},{12,8},{13,9},{14,12},{15,13},... | collective-permute-start | bytes 1572872 | tf_op jit(solution)/shard_map/project_in/ppermute | solution.py:492
  19.3 11.9 %collective-permute-start.7 = (bf16[2048,256]{1,0:T(8,128)(2,1)}, bf16[2048,256]{1,0:T(8,128)(2,1)S(1)}, u32[]{:S(2)}, u32[]{:S(2)}) collective-permute-start(bf16[2048,256]{1,0:T(8,128)(2,1)} %param.21), channel_id=1, source_target_pairs={{0,1},{1,0},{2,3},{3,2},{4,5},{5,4},{6,7},{7,6},{8,9},{9,8},{10,11... | collective-permute-start | bytes 3145736 | tf_op jit(solution)/shard_map/head_weights/ppermute | solution.py:496
  19.3 11.3 %collective-permute-start.6 = (bf16[2048,256]{1,0:T(8,128)(2,1)}, bf16[2048,256]{1,0:T(8,128)(2,1)S(1)}, u32[]{:S(2)}, u32[]{:S(2)}) collective-permute-start(bf16[2048,256]{1,0:T(8,128)(2,1)} %param.20), channel_id=1, source_target_pairs={{0,1},{1,0},{2,3},{3,2},{4,5},{5,4},{6,7},{7,6},{8,9},{9,8},{10,11... | collective-permute-start | bytes 3145736 | tf_op jit(solution)/shard_map/head_weights/ppermute | solution.py:496
  30.6 16.9 %collective-permute-start.10 = (bf16[256,2048]{1,0:T(8,128)(2,1)S(1)}, bf16[256,2048]{1,0:T(8,128)(2,1)S(1)}, u32[]{:S(2)}, u32[]{:S(2)}) collective-permute-start(bf16[256,2048]{1,0:T(8,128)(2,1)S(1)} %copy-done.120), channel_id=1, source_target_pairs={{0,1},{1,0},{2,3},{3,2},{4,5},{5,4},{6,7},{7,6},{8,9},{9,8},{10,11... | collective-permute-start | bytes 3145736 | tf_op jit(solution)/shard_map/head_weights/ppermute | solution.py:496
  31.8 14.4 %collective-permute-start.8 = (bf16[128,2048]{1,0:T(8,128)(2,1)S(1)}, bf16[128,2048]{1,0:T(8,128)(2,1)S(1)}, u32[]{:S(2)}, u32[]{:S(2)}) collective-permute-start(bf16[128,2048]{1,0:T(8,128)(2,1)S(1)} %collective-permute-done.2.refs_3_), channel_id=1, source_target_pairs={{0,4},{1,5},{4,8},{5,9},{8,12},{9,13},{12,14},{13,15},{14,10},{15,... | collective-permute-start | bytes 1572872 | tf_op jit(solution)/shard_map/project_in/ppermute | solution.py:492
  33.4 14.0 %collective-permute-start.9 = (bf16[128,2048]{1,0:T(8,128)(2,1)S(1)}, bf16[128,2048]{1,0:T(8,128)(2,1)S(1)}, u32[]{:S(2)}, u32[]{:S(2)}) collective-permute-start(bf16[128,2048]{1,0:T(8,128)(2,1)S(1)} %collective-permute-done.3.refs_4_), channel_id=1, source_target_pairs={{0,2},{1,3},{4,0},{5,1},{8,4},{9,5},{12,8},{13,9},{14,12},{15,13},... | collective-permute-start | bytes 1572872 | tf_op jit(solution)/shard_map/project_in/ppermute | solution.py:492
  59.3 22.5 %collective-permute-start.19 = (bf16[128,2048]{1,0:T(8,128)(2,1)S(1)}, bf16[128,2048]{1,0:T(8,128)(2,1)}, u32[]{:S(2)}, u32[]{:S(2)}) collective-permute-start(bf16[128,2048]{1,0:T(8,128)(2,1)S(1)} %copy-done.72), channel_id=1, source_target_pairs={{0,2},{1,3},{4,0},{5,1},{8,4},{9,5},{12,8},{13,9},{14,12},{15,13},... | collective-permute-start | bytes 1572872 | tf_op jit(solution)/shard_map/gather_out_grad/ppermute | solution.py:492
  59.8 22.0 %collective-permute-start.18 = (bf16[128,2048]{1,0:T(8,128)(2,1)S(1)}, bf16[128,2048]{1,0:T(8,128)(2,1)}, u32[]{:S(2)}, u32[]{:S(2)}) collective-permute-start(bf16[128,2048]{1,0:T(8,128)(2,1)S(1)} %copy-done.72), channel_id=1, source_target_pairs={{0,4},{1,5},{4,8},{5,9},{8,12},{9,13},{12,14},{13,15},{14,10},{15,... | collective-permute-start | bytes 1572872 | tf_op jit(solution)/shard_map/gather_out_grad/ppermute | solution.py:492
  63.3 16.2 %collective-permute-start.16 = (bf16[128,1024]{1,0:T(8,128)(2,1)S(1)}, bf16[128,1024]{1,0:T(8,128)(2,1)S(1)}, u32[]{:S(2)}, u32[]{:S(2)}) collective-permute-start(bf16[128,1024]{1,0:T(8,128)(2,1)S(1)} %get-tuple-element.343), channel_id=1, source_target_pairs={{0,4},{1,5},{4,8},{5,9},{8,12},{9,13},{12,14},{13,15},{14,10},{15,... | collective-permute-start | bytes 786440 | tf_op jit(solution)/shard_map/retention/ppermute | solution.py:492
  64.8 14.6 %collective-permute-start.17 = (bf16[128,1024]{1,0:T(8,128)(2,1)S(1)}, bf16[128,1024]{1,0:T(8,128)(2,1)S(1)}, u32[]{:S(2)}, u32[]{:S(2)}) collective-permute-start(bf16[128,1024]{1,0:T(8,128)(2,1)S(1)} %get-tuple-element.344), channel_id=1, source_target_pairs={{0,2},{1,3},{4,0},{5,1},{8,4},{9,5},{12,8},{13,9},{14,12},{15,13},... | collective-permute-start | bytes 786440 | tf_op jit(solution)/shard_map/retention/ppermute | solution.py:492
  79.7 13.4 %collective-permute-start.20 = (bf16[128,2048]{1,0:T(8,128)(2,1)S(1)}, bf16[128,2048]{1,0:T(8,128)(2,1)S(1)}, u32[]{:S(2)}, u32[]{:S(2)}) collective-permute-start(bf16[128,2048]{1,0:T(8,128)(2,1)S(1)} %pad_maximum_fusion.4), channel_id=1, source_target_pairs={{0,4},{1,5},{4,8},{5,9},{8,12},{9,13},{12,14},{13,15},{14,10},{15,... | collective-permute-start | bytes 1572872 | tf_op jit(solution)/shard_map/retention/ppermute | solution.py:492
  81.4 13.0 %collective-permute-start.21 = (bf16[128,2048]{1,0:T(8,128)(2,1)S(1)}, bf16[128,2048]{1,0:T(8,128)(2,1)S(1)}, u32[]{:S(2)}, u32[]{:S(2)}) collective-permute-start(bf16[128,2048]{1,0:T(8,128)(2,1)S(1)} %pad_maximum_fusion.5), channel_id=1, source_target_pairs={{0,2},{1,3},{4,0},{5,1},{8,4},{9,5},{12,8},{13,9},{14,12},{15,13},... | collective-permute-start | bytes 1572872 | tf_op jit(solution)/shard_map/retention/ppermute | solution.py:492
  94.7 14.9 %collective-permute-start.22 = (bf16[128,2048]{1,0:T(8,128)(2,1)S(1)}, bf16[128,2048]{1,0:T(8,128)(2,1)S(1)}, u32[]{:S(2)}, u32[]{:S(2)}) collective-permute-start(bf16[128,2048]{1,0:T(8,128)(2,1)S(1)} %get-tuple-element.362), channel_id=1, source_target_pairs={{0,4},{1,5},{4,8},{5,9},{8,12},{9,13},{12,14},{13,15},{14,10},{15,... | collective-permute-start | bytes 1572872 | tf_op jit(solution)/shard_map/retention/ppermute | solution.py:492
  96.2 14.9 %collective-permute-start.23 = (bf16[128,2048]{1,0:T(8,128)(2,1)S(1)}, bf16[128,2048]{1,0:T(8,128)(2,1)S(1)}, u32[]{:S(2)}, u32[]{:S(2)}) collective-permute-start(bf16[128,2048]{1,0:T(8,128)(2,1)S(1)} %get-tuple-element.363), channel_id=1, source_target_pairs={{0,2},{1,3},{4,0},{5,1},{8,4},{9,5},{12,8},{13,9},{14,12},{15,13},... | collective-permute-start | bytes 1572872 | tf_op jit(solution)/shard_map/retention/ppermute | solution.py:492
  96.8 24.2 %collective-permute-start.30 = (bf16[128,2048]{1,0:T(8,128)(2,1)}, bf16[128,2048]{1,0:T(8,128)(2,1)}, u32[]{:S(2)}, u32[]{:S(2)}) collective-permute-start(bf16[128,2048]{1,0:T(8,128)(2,1)} %collective-permute-done.18.refs_6_), channel_id=1, source_target_pairs={{0,4},{1,5},{4,8},{5,9},{8,12},{9,13},{12,14},{13,15},{14,10},{15,... | collective-permute-start | bytes 1572872 | tf_op jit(solution)/shard_map/gather_out_grad/ppermute | solution.py:492
  98.3 24.2 %collective-permute-start.31 = (bf16[128,2048]{1,0:T(8,128)(2,1)}, bf16[128,2048]{1,0:T(8,128)(2,1)}, u32[]{:S(2)}, u32[]{:S(2)}) collective-permute-start(bf16[128,2048]{1,0:T(8,128)(2,1)} %collective-permute-done.19.refs_7_), channel_id=1, source_target_pairs={{0,2},{1,3},{4,0},{5,1},{8,4},{9,5},{12,8},{13,9},{14,12},{15,13},... | collective-permute-start | bytes 1572872 | tf_op jit(solution)/shard_map/gather_out_grad/ppermute | solution.py:492
  112.5 19.8 %collective-permute-start.24 = (bf16[128,2048]{1,0:T(8,128)(2,1)}, bf16[128,2048]{1,0:T(8,128)(2,1)}, u32[]{:S(2)}, u32[]{:S(2)}) collective-permute-start(bf16[128,2048]{1,0:T(8,128)(2,1)} %get-tuple-element.366), channel_id=1, source_target_pairs={{0,4},{1,5},{4,8},{5,9},{8,12},{9,13},{12,14},{13,15},{14,10},{15,... | collective-permute-start | bytes 1572872 | tf_op jit(solution)/shard_map/retention/ppermute | solution.py:492
  113.4 19.3 %collective-permute-start.25 = (bf16[128,2048]{1,0:T(8,128)(2,1)}, bf16[128,2048]{1,0:T(8,128)(2,1)}, u32[]{:S(2)}, u32[]{:S(2)}) collective-permute-start(bf16[128,2048]{1,0:T(8,128)(2,1)} %get-tuple-element.367), channel_id=1, source_target_pairs={{0,2},{1,3},{4,0},{5,1},{8,4},{9,5},{12,8},{13,9},{14,12},{15,13},... | collective-permute-start | bytes 1572872 | tf_op jit(solution)/shard_map/retention/ppermute | solution.py:492
  114.5 21.3 %collective-permute-start.32 = (bf16[2048,256]{1,0:T(8,128)(2,1)}, bf16[2048,256]{1,0:T(8,128)(2,1)S(1)}, u32[]{:S(2)}, u32[]{:S(2)}) collective-permute-start(bf16[2048,256]{1,0:T(8,128)(2,1)} %param.23), channel_id=1, source_target_pairs={{0,1},{1,0},{2,3},{3,2},{4,5},{5,4},{6,7},{7,6},{8,9},{9,8},{10,11... | collective-permute-start | bytes 3145736 | tf_op jit(solution)/shard_map/feed_weights/ppermute | solution.py:496
  121.0 34.0 %collective-permute-start.33 = (bf16[256,2048]{1,0:T(8,128)(2,1)}, bf16[256,2048]{1,0:T(8,128)(2,1)S(1)}, u32[]{:S(2)}, u32[]{:S(2)}) collective-permute-start(bf16[256,2048]{1,0:T(8,128)(2,1)} %param.24), channel_id=1, source_target_pairs={{0,1},{1,0},{2,3},{3,2},{4,5},{5,4},{6,7},{7,6},{8,9},{9,8},{10,11... | collective-permute-start | bytes 3145736 | tf_op jit(solution)/shard_map/feed_weights/ppermute | solution.py:496
  122.4 32.7 %collective-permute-start.36 = (bf16[128,2048]{1,0:T(8,128)(2,1)}, bf16[128,2048]{1,0:T(8,128)(2,1)S(1)}, u32[]{:S(2)}, u32[]{:S(2)}) collective-permute-start(bf16[128,2048]{1,0:T(8,128)(2,1)} %collective-permute-done.30.refs_8_), channel_id=1, source_target_pairs={{0,4},{1,5},{4,8},{5,9},{8,12},{9,13},{12,14},{13,15},{14,10},{15,... | collective-permute-start | bytes 1572872 | tf_op jit(solution)/shard_map/gather_out_grad/ppermute | solution.py:492
  132.2 22.9 %collective-permute-start.37 = (bf16[128,2048]{1,0:T(8,128)(2,1)}, bf16[128,2048]{1,0:T(8,128)(2,1)S(1)}, u32[]{:S(2)}, u32[]{:S(2)}) collective-permute-start(bf16[128,2048]{1,0:T(8,128)(2,1)} %collective-permute-done.31.refs_9_), channel_id=1, source_target_pairs={{0,2},{1,3},{4,0},{5,1},{8,4},{9,5},{12,8},{13,9},{14,12},{15,13},... | collective-permute-start | bytes 1572872 | tf_op jit(solution)/shard_map/gather_out_grad/ppermute | solution.py:492
  135.3 17.7 %collective-permute-start.27 = (bf16[128,2048]{1,0:T(8,128)(2,1)S(1)}, bf16[128,2048]{1,0:T(8,128)(2,1)S(1)}, u32[]{:S(2)}, u32[]{:S(2)}) collective-permute-start(bf16[128,2048]{1,0:T(8,128)(2,1)S(1)} %add_convert_fusion.6.refs_0_), channel_id=1, source_target_pairs={{0,2},{1,3},{4,0},{5,1},{8,4},{9,5},{12,8},{13,9},{14,12},{15,13},... | collective-permute-start | bytes 1572872 | tf_op jit(solution)/shard_map/feed_forward/ppermute | solution.py:492
  135.8 17.2 %collective-permute-start.26 = (bf16[128,2048]{1,0:T(8,128)(2,1)S(1)}, bf16[128,2048]{1,0:T(8,128)(2,1)S(1)}, u32[]{:S(2)}, u32[]{:S(2)}) collective-permute-start(bf16[128,2048]{1,0:T(8,128)(2,1)S(1)} %add_convert_fusion.6.refs_0_), channel_id=1, source_target_pairs={{0,4},{1,5},{4,8},{5,9},{8,12},{9,13},{12,14},{13,15},{14,10},{15,... | collective-permute-start | bytes 1572872 | tf_op jit(solution)/shard_map/feed_forward/ppermute | solution.py:492
  153.0 14.9 %collective-permute-start.28 = (bf16[128,2048]{1,0:T(8,128)(2,1)S(1)}, bf16[128,2048]{1,0:T(8,128)(2,1)S(1)}, u32[]{:S(2)}, u32[]{:S(2)}) collective-permute-start(bf16[128,2048]{1,0:T(8,128)(2,1)S(1)} %collective-permute-done.26.refs_1_), channel_id=1, source_target_pairs={{0,4},{1,5},{4,8},{5,9},{8,12},{9,13},{12,14},{13,15},{14,10},{15,... | collective-permute-start | bytes 1572872 | tf_op jit(solution)/shard_map/feed_forward/ppermute | solution.py:492
  154.0 14.9 %collective-permute-start.29 = (bf16[128,2048]{1,0:T(8,128)(2,1)S(1)}, bf16[128,2048]{1,0:T(8,128)(2,1)S(1)}, u32[]{:S(2)}, u32[]{:S(2)}) collective-permute-start(bf16[128,2048]{1,0:T(8,128)(2,1)S(1)} %collective-permute-done.27.refs_2_), channel_id=1, source_target_pairs={{0,2},{1,3},{4,0},{5,1},{8,4},{9,5},{12,8},{13,9},{14,12},{15,13},... | collective-permute-start | bytes 1572872 | tf_op jit(solution)/shard_map/feed_forward/ppermute | solution.py:492
  155.2 18.2 %collective-permute-start.40 = (bf16[128,1024]{1,0:T(8,128)(2,1)S(1)}, bf16[128,1024]{1,0:T(8,128)(2,1)S(1)}, u32[]{:S(2)}, u32[]{:S(2)}) collective-permute-start(bf16[128,1024]{1,0:T(8,128)(2,1)S(1)} %slice.170), channel_id=1, source_target_pairs={{0,4},{1,5},{4,8},{5,9},{8,12},{9,13},{12,14},{13,15},{14,10},{15,... | collective-permute-start | bytes 786440 | tf_op jit(solution)/shard_map/gather_out_grad/ppermute | solution.py:492
  156.3 18.2 %collective-permute-start.41 = (bf16[128,1024]{1,0:T(8,128)(2,1)S(1)}, bf16[128,1024]{1,0:T(8,128)(2,1)S(1)}, u32[]{:S(2)}, u32[]{:S(2)}) collective-permute-start(bf16[128,1024]{1,0:T(8,128)(2,1)S(1)} %slice.171), channel_id=1, source_target_pairs={{0,2},{1,3},{4,0},{5,1},{8,4},{9,5},{12,8},{13,9},{14,12},{15,13},... | collective-permute-start | bytes 786440 | tf_op jit(solution)/shard_map/gather_out_grad/ppermute | solution.py:492
  168.8 13.4 %collective-permute-start.34 = (bf16[128,2048]{1,0:T(8,128)(2,1)S(1)}, bf16[128,2048]{1,0:T(8,128)(2,1)S(1)}, u32[]{:S(2)}, u32[]{:S(2)}) collective-permute-start(bf16[128,2048]{1,0:T(8,128)(2,1)S(1)} %collective-permute-done.28.refs_3_), channel_id=1, source_target_pairs={{0,4},{1,5},{4,8},{5,9},{8,12},{9,13},{12,14},{13,15},{14,10},{15,... | collective-permute-start | bytes 1572872 | tf_op jit(solution)/shard_map/feed_forward/ppermute | solution.py:492
  169.4 12.8 %collective-permute-start.35 = (bf16[128,2048]{1,0:T(8,128)(2,1)S(1)}, bf16[128,2048]{1,0:T(8,128)(2,1)S(1)}, u32[]{:S(2)}, u32[]{:S(2)}) collective-permute-start(bf16[128,2048]{1,0:T(8,128)(2,1)S(1)} %collective-permute-done.29.refs_4_), channel_id=1, source_target_pairs={{0,2},{1,3},{4,0},{5,1},{8,4},{9,5},{12,8},{13,9},{14,12},{15,13},... | collective-permute-start | bytes 1572872 | tf_op jit(solution)/shard_map/feed_forward/ppermute | solution.py:492
  196.2 20.2 %collective-permute-start.45 = (bf16[2048,256]{1,0:T(8,128)(2,1)S(1)}, bf16[2048,256]{1,0:T(8,128)(2,1)S(1)}, u32[]{:S(2)}, u32[]{:S(2)}) collective-permute-start(bf16[2048,256]{1,0:T(8,128)(2,1)S(1)} %convolution_convert_fusion), channel_id=1, source_target_pairs={{0,1},{1,0},{2,3},{3,2},{4,5},{5,4},{6,7},{7,6},{8,9},{9,8},{10,11... | collective-permute-start | bytes 3145736 | tf_op jit(solution)/shard_map/scatter_up/down_grad/ppermute | solution.py:496
  199.5 11.6 %collective-permute-start.47 = (bf16[128,2048]{1,0:T(8,128)(2,1)S(1)}, bf16[128,2048]{1,0:T(8,128)(2,1)S(1)}, u32[]{:S(2)}, u32[]{:S(2)}) collective-permute-start(bf16[128,2048]{1,0:T(8,128)(2,1)S(1)} %pad_maximum_fusion.6), channel_id=1, source_target_pairs={{0,4},{1,5},{4,8},{5,9},{8,12},{9,13},{12,14},{13,15},{14,10},{15,... | collective-permute-start | bytes 1572872 | tf_op jit(solution)/shard_map/scatter_up/ppermute | solution.py:492
  200.1 11.4 %collective-permute-start.48 = (bf16[128,2048]{1,0:T(8,128)(2,1)S(1)}, bf16[128,2048]{1,0:T(8,128)(2,1)S(1)}, u32[]{:S(2)}, u32[]{:S(2)}) collective-permute-start(bf16[128,2048]{1,0:T(8,128)(2,1)S(1)} %pad_maximum_fusion.7), channel_id=1, source_target_pairs={{0,2},{1,3},{4,0},{5,1},{8,4},{9,5},{12,8},{13,9},{14,12},{15,13},... | collective-permute-start | bytes 1572872 | tf_op jit(solution)/shard_map/scatter_up/ppermute | solution.py:492
  203.5 22.9 %collective-permute-start.44 = (bf16[2048,256]{1,0:T(8,128)(2,1)S(1)}, bf16[2048,256]{1,0:T(8,128)(2,1)S(1)}, u32[]{:S(2)}, u32[]{:S(2)}) collective-permute-start(bf16[2048,256]{1,0:T(8,128)(2,1)S(1)} %convolution_convert_fusion.1), channel_id=1, source_target_pairs={{0,1},{1,0},{2,3},{3,2},{4,5},{5,4},{6,7},{7,6},{8,9},{9,8},{10,11... | collective-permute-start | bytes 3145736 | tf_op jit(solution)/shard_map/scatter_up/up_grad/ppermute | solution.py:496
  211.9 11.7 %collective-permute-start.49 = (bf16[128,2048]{1,0:T(8,128)(2,1)S(1)}, bf16[128,2048]{1,0:T(8,128)(2,1)S(1)}, u32[]{:S(2)}, u32[]{:S(2)}) collective-permute-start(bf16[128,2048]{1,0:T(8,128)(2,1)S(1)} %get-tuple-element.442), channel_id=1, source_target_pairs={{0,4},{1,5},{4,8},{5,9},{8,12},{9,13},{12,14},{13,15},{14,10},{15,... | collective-permute-start | bytes 1572872 | tf_op jit(solution)/shard_map/scatter_up/ppermute | solution.py:492
  212.6 11.4 %collective-permute-start.50 = (bf16[128,2048]{1,0:T(8,128)(2,1)S(1)}, bf16[128,2048]{1,0:T(8,128)(2,1)S(1)}, u32[]{:S(2)}, u32[]{:S(2)}) collective-permute-start(bf16[128,2048]{1,0:T(8,128)(2,1)S(1)} %get-tuple-element.443), channel_id=1, source_target_pairs={{0,2},{1,3},{4,0},{5,1},{8,4},{9,5},{12,8},{13,9},{14,12},{15,13},... | collective-permute-start | bytes 1572872 | tf_op jit(solution)/shard_map/scatter_up/ppermute | solution.py:492
  224.4 9.2 %collective-permute-start.51 = (bf16[128,2048]{1,0:T(8,128)(2,1)S(1)}, bf16[128,2048]{1,0:T(8,128)(2,1)S(1)}, u32[]{:S(2)}, u32[]{:S(2)}) collective-permute-start(bf16[128,2048]{1,0:T(8,128)(2,1)S(1)} %get-tuple-element.446), channel_id=1, source_target_pairs={{0,4},{1,5},{4,8},{5,9},{8,12},{9,13},{12,14},{13,15},{14,10},{15,... | collective-permute-start | bytes 1572872 | tf_op jit(solution)/shard_map/scatter_up/ppermute | solution.py:492
  225.0 9.8 %collective-permute-start.52 = (bf16[128,2048]{1,0:T(8,128)(2,1)S(1)}, bf16[128,2048]{1,0:T(8,128)(2,1)S(1)}, u32[]{:S(2)}, u32[]{:S(2)}) collective-permute-start(bf16[128,2048]{1,0:T(8,128)(2,1)S(1)} %get-tuple-element.447), channel_id=1, source_target_pairs={{0,2},{1,3},{4,0},{5,1},{8,4},{9,5},{12,8},{13,9},{14,12},{15,13},... | collective-permute-start | bytes 1572872 | tf_op jit(solution)/shard_map/scatter_up/ppermute | solution.py:492
  237.4 12.7 %collective-permute-start.54 = (bf16[128,2048]{1,0:T(8,128)(2,1)S(1)}, bf16[128,2048]{1,0:T(8,128)(2,1)S(1)}, u32[]{:S(2)}, u32[]{:S(2)}) collective-permute-start(bf16[128,2048]{1,0:T(8,128)(2,1)S(1)} %get-tuple-element.464.refs_0_), channel_id=1, source_target_pairs={{0,2},{1,3},{4,0},{5,1},{8,4},{9,5},{12,8},{13,9},{14,12},{15,13},... | collective-permute-start | bytes 1572872 | tf_op jit(solution)/shard_map/gate_back/ppermute | solution.py:492
  238.9 14.7 %collective-permute-start.53 = (bf16[128,2048]{1,0:T(8,128)(2,1)S(1)}, bf16[128,2048]{1,0:T(8,128)(2,1)S(1)}, u32[]{:S(2)}, u32[]{:S(2)}) collective-permute-start(bf16[128,2048]{1,0:T(8,128)(2,1)S(1)} %get-tuple-element.464.refs_0_), channel_id=1, source_target_pairs={{0,4},{1,5},{4,8},{5,9},{8,12},{9,13},{12,14},{13,15},{14,10},{15,... | collective-permute-start | bytes 1572872 | tf_op jit(solution)/shard_map/gate_back/ppermute | solution.py:492
  239.4 52.2 %collective-permute-start.46 = (bf16[2048,512]{1,0:T(8,128)(2,1)S(1)}, bf16[2048,512]{1,0:T(8,128)(2,1)S(1)}, u32[]{:S(2)}, u32[]{:S(2)}) collective-permute-start(bf16[2048,512]{1,0:T(8,128)(2,1)S(1)} %pad_maximum_fusion.3.refs_0_), channel_id=1, source_target_pairs={{0,16},{16,0},{1,17},{17,1},{2,18},{18,2},{3,19},{19,3},{4,20},{20... | collective-permute-start | bytes 6291464 | tf_op jit(solution)/shard_map/feed_grads/ppermute | solution.py:761
  253.6 14.1 %collective-permute-start.55 = (bf16[128,2048]{1,0:T(8,128)(2,1)S(1)}, bf16[128,2048]{1,0:T(8,128)(2,1)S(1)}, u32[]{:S(2)}, u32[]{:S(2)}) collective-permute-start(bf16[128,2048]{1,0:T(8,128)(2,1)S(1)} %collective-permute-done.53.refs_1_), channel_id=1, source_target_pairs={{0,4},{1,5},{4,8},{5,9},{8,12},{9,13},{12,14},{13,15},{14,10},{15,... | collective-permute-start | bytes 1572872 | tf_op jit(solution)/shard_map/gate_back/ppermute | solution.py:492
  254.0 14.1 %collective-permute-start.56 = (bf16[128,2048]{1,0:T(8,128)(2,1)S(1)}, bf16[128,2048]{1,0:T(8,128)(2,1)S(1)}, u32[]{:S(2)}, u32[]{:S(2)}) collective-permute-start(bf16[128,2048]{1,0:T(8,128)(2,1)S(1)} %collective-permute-done.54.refs_2_), channel_id=1, source_target_pairs={{0,2},{1,3},{4,0},{5,1},{8,4},{9,5},{12,8},{13,9},{14,12},{15,13},... | collective-permute-start | bytes 1572872 | tf_op jit(solution)/shard_map/gate_back/ppermute | solution.py:492
  269.1 9.4 %collective-permute-start.58 = (bf16[128,2048]{1,0:T(8,128)(2,1)S(1)}, bf16[128,2048]{1,0:T(8,128)(2,1)S(1)}, u32[]{:S(2)}, u32[]{:S(2)}) collective-permute-start(bf16[128,2048]{1,0:T(8,128)(2,1)S(1)} %collective-permute-done.56.refs_4_), channel_id=1, source_target_pairs={{0,2},{1,3},{4,0},{5,1},{8,4},{9,5},{12,8},{13,9},{14,12},{15,13},... | collective-permute-start | bytes 1572872 | tf_op jit(solution)/shard_map/gate_back/ppermute | solution.py:492
  291.0 27.2 %collective-permute-start.68 = (bf16[256,2048]{1,0:T(8,128)(2,1)S(1)}, bf16[256,2048]{1,0:T(8,128)(2,1)S(1)}, u32[]{:S(2)}, u32[]{:S(2)}) collective-permute-start(bf16[256,2048]{1,0:T(8,128)(2,1)S(1)} %product_shard.8), channel_id=1, source_target_pairs={{0,1},{1,0},{2,3},{3,2},{4,5},{5,4},{6,7},{7,6},{8,9},{9,8},{10,11... | collective-permute-start | bytes 3145736 | tf_op jit(solution)/shard_map/out_grad/ppermute | solution.py:496
  299.3 14.0 %collective-permute-start.64 = (bf16[256,1024]{1,0:T(8,128)(2,1)S(1)}, bf16[256,1024]{1,0:T(8,128)(2,1)S(1)}, u32[]{:S(2)}, u32[]{:S(2)}) collective-permute-start(bf16[256,1024]{1,0:T(8,128)(2,1)S(1)} %pad_maximum_fusion.8), channel_id=1, source_target_pairs={{0,4},{1,5},{4,8},{5,9},{8,12},{9,13},{12,14},{13,15},{14,10},{15,... | collective-permute-start | bytes 1572872 | tf_op jit(solution)/shard_map/key_back/ppermute | solution.py:492
  300.9 14.1 %collective-permute-start.65 = (bf16[256,1024]{1,0:T(8,128)(2,1)S(1)}, bf16[256,1024]{1,0:T(8,128)(2,1)S(1)}, u32[]{:S(2)}, u32[]{:S(2)}) collective-permute-start(bf16[256,1024]{1,0:T(8,128)(2,1)S(1)} %pad_maximum_fusion.9), channel_id=1, source_target_pairs={{0,2},{1,3},{4,0},{5,1},{8,4},{9,5},{12,8},{13,9},{14,12},{15,13},... | collective-permute-start | bytes 1572872 | tf_op jit(solution)/shard_map/key_back/ppermute | solution.py:492
  304.5 21.6 %collective-permute-start.70 = (bf16[2048,256]{1,0:T(8,128)(2,1)S(1)}, bf16[2048,256]{1,0:T(8,128)(2,1)S(1)}, u32[]{:S(2)}, u32[]{:S(2)}) collective-permute-start(bf16[2048,256]{1,0:T(8,128)(2,1)S(1)} %product_shard.10), channel_id=1, source_target_pairs={{0,1},{1,0},{2,3},{3,2},{4,5},{5,4},{6,7},{7,6},{8,9},{9,8},{10,11... | collective-permute-start | bytes 3145736 | tf_op jit(solution)/shard_map/key_back/gate_grad/ppermute | solution.py:496
  316.1 25.2 %collective-permute-start.66 = (bf16[256,2048]{1,0:T(8,128)(2,1)}, bf16[256,2048]{1,0:T(8,128)(2,1)S(1)}, u32[]{:S(2)}, u32[]{:S(2)}) collective-permute-start(bf16[256,2048]{1,0:T(8,128)(2,1)} %get-tuple-element.514), channel_id=1, source_target_pairs={{0,4},{1,5},{4,8},{5,9},{8,12},{9,13},{12,14},{13,15},{14,10},{15,... | collective-permute-start | bytes 3145736 | tf_op jit(solution)/shard_map/key_back/ppermute | solution.py:492
  316.9 24.4 %collective-permute-start.67 = (bf16[256,2048]{1,0:T(8,128)(2,1)S(1)}, bf16[256,2048]{1,0:T(8,128)(2,1)S(1)}, u32[]{:S(2)}, u32[]{:S(2)}) collective-permute-start(bf16[256,2048]{1,0:T(8,128)(2,1)S(1)} %get-tuple-element.515), channel_id=1, source_target_pairs={{0,2},{1,3},{4,0},{5,1},{8,4},{9,5},{12,8},{13,9},{14,12},{15,13},... | collective-permute-start | bytes 3145736 | tf_op jit(solution)/shard_map/key_back/ppermute | solution.py:492
  320.9 23.6 %collective-permute-start.69 = (bf16[256,2048]{1,0:T(8,128)(2,1)S(1)}, bf16[256,2048]{1,0:T(8,128)(2,1)S(1)}, u32[]{:S(2)}, u32[]{:S(2)}) collective-permute-start(bf16[256,2048]{1,0:T(8,128)(2,1)S(1)} %product_shard.9.refs_0_), channel_id=1, source_target_pairs={{0,16},{16,0},{1,17},{17,1},{2,18},{18,2},{3,19},{19,3},{4,20},{20... | collective-permute-start | bytes 3145736 | tf_op jit(solution)/shard_map/key_back/out_grad/ppermute | solution.py:761
  347.8 25.6 %collective-permute-start.71 = (bf16[256,2048]{1,0:T(8,128)(2,1)S(1)}, bf16[256,2048]{1,0:T(8,128)(2,1)S(1)}, u32[]{:S(2)}, u32[]{:S(2)}) collective-permute-start(bf16[256,2048]{1,0:T(8,128)(2,1)S(1)} %get-tuple-element.539), channel_id=1, source_target_pairs={{0,4},{1,5},{4,8},{5,9},{8,12},{9,13},{12,14},{13,15},{14,10},{15,... | collective-permute-start | bytes 3145736 | tf_op jit(solution)/shard_map/key_back/ppermute | solution.py:492
  348.6 25.2 %collective-permute-start.72 = (bf16[256,2048]{1,0:T(8,128)(2,1)S(1)}, bf16[256,2048]{1,0:T(8,128)(2,1)S(1)}, u32[]{:S(2)}, u32[]{:S(2)}) collective-permute-start(bf16[256,2048]{1,0:T(8,128)(2,1)S(1)} %get-tuple-element.540), channel_id=1, source_target_pairs={{0,2},{1,3},{4,0},{5,1},{8,4},{9,5},{12,8},{13,9},{14,12},{15,13},... | collective-permute-start | bytes 3145736 | tf_op jit(solution)/shard_map/key_back/ppermute | solution.py:492
  349.9 31.1 %collective-permute-start.77 = (bf16[2048,256]{1,0:T(8,128)(2,1)S(1)}, bf16[2048,256]{1,0:T(8,128)(2,1)S(1)}, u32[]{:S(2)}, u32[]{:S(2)}) collective-permute-start(bf16[2048,256]{1,0:T(8,128)(2,1)S(1)} %product_shard.11.refs_0_), channel_id=1, source_target_pairs={{0,16},{16,0},{1,17},{17,1},{2,18},{18,2},{3,19},{19,3},{4,20},{20... | collective-permute-start | bytes 3145736 | tf_op jit(solution)/shard_map/key_back/ppermute | solution.py:761
  354.4 26.5 %collective-permute-start.78 = (bf16[2048,256]{1,0:T(8,128)(2,1)S(1)}, bf16[2048,256]{1,0:T(8,128)(2,1)S(1)}, u32[]{:S(2)}, u32[]{:S(2)}) collective-permute-start(bf16[2048,256]{1,0:T(8,128)(2,1)S(1)} %product_shard.14), channel_id=1, source_target_pairs={{0,1},{1,0},{2,3},{3,2},{4,5},{5,4},{6,7},{7,6},{8,9},{9,8},{10,11... | collective-permute-start | bytes 3145736 | tf_op jit(solution)/shard_map/key_back/query_key_grad/ppermute | solution.py:496
  357.3 42.5 %collective-permute-start.76 = (bf16[2048,256]{1,0:T(8,128)(2,1)S(1)}, bf16[2048,256]{1,0:T(8,128)(2,1)S(1)}, u32[]{:S(2)}, u32[]{:S(2)}) collective-permute-start(bf16[2048,256]{1,0:T(8,128)(2,1)S(1)} %product_shard.13.refs_0_), channel_id=1, source_target_pairs={{0,16},{16,0},{1,17},{17,1},{2,18},{18,2},{3,19},{19,3},{4,20},{20... | collective-permute-start | bytes 3145736 | tf_op jit(solution)/shard_map/key_back/value_grad/ppermute | solution.py:761
  374.4 24.5 %collective-permute-start.74 = (bf16[256,2048]{1,0:T(8,128)(2,1)S(1)}, bf16[256,2048]{1,0:T(8,128)(2,1)S(1)}, u32[]{:S(2)}, u32[]{:S(2)}) collective-permute-start(bf16[256,2048]{1,0:T(8,128)(2,1)S(1)} %get-tuple-element.552), channel_id=1, source_target_pairs={{0,4},{1,5},{4,8},{5,9},{8,12},{9,13},{12,14},{13,15},{14,10},{15,... | collective-permute-start | bytes 3145736 | tf_op jit(solution)/shard_map/key_back/ppermute | solution.py:492
  375.4 24.3 %collective-permute-start.75 = (bf16[256,2048]{1,0:T(8,128)(2,1)S(1)}, bf16[256,2048]{1,0:T(8,128)(2,1)S(1)}, u32[]{:S(2)}, u32[]{:S(2)}) collective-permute-start(bf16[256,2048]{1,0:T(8,128)(2,1)S(1)} %get-tuple-element.553), channel_id=1, source_target_pairs={{0,2},{1,3},{4,0},{5,1},{8,4},{9,5},{12,8},{13,9},{14,12},{15,13},... | collective-permute-start | bytes 3145736 | tf_op jit(solution)/shard_map/key_back/ppermute | solution.py:492
  383.8 35.9 %collective-permute-start.79 = (bf16[2048,256]{1,0:T(8,128)(2,1)S(1)}, bf16[2048,256]{1,0:T(8,128)(2,1)S(1)}, u32[]{:S(2)}, u32[]{:S(2)}) collective-permute-start(bf16[2048,256]{1,0:T(8,128)(2,1)S(1)} %product_shard.15.refs_0_), channel_id=1, source_target_pairs={{0,16},{16,0},{1,17},{17,1},{2,18},{18,2},{3,19},{19,3},{4,20},{20... | collective-permute-start | bytes 3145736 | tf_op jit(solution)/shard_map/key_back/query_key_grad/ppermute | solution.py:761
  (154 other events, 1784.4 us)
where the time goes:
time: 429 us; the launch traced here: 422 us
  waiting for transfers between devices  197 us (46%)
  Pallas kernels  109 us (25%)
  starting transfers between devices  75.2 us (18%)
  other arithmetic  15.1 us (4%)
  local copies, waits for them, and re-layouts  13.2 us (3%)
  matrix products  9.39 us (2%)
    ppermute x56, waiting for transfers between devices, ring_shift(): return lax.ppermute(value, 'mp', pairs)  185 us
    pallas_call x28, Pallas kernels, run(): pl.pallas_call(kernel, out_shape=[jax.ShapeDtypeStruct(shape, dtype) for...  86.8 us
    ppermute x56, starting transfers between devices, ring_shift(): return lax.ppermute(value, 'mp', pairs)  59.7 us
    pallas_call x8, Pallas kernels, product_shard(): pl.pallas_call(kernel, grid_spec=pltpu.PrefetchScalarGridSpec(num_scalar_...  22 us
  transfers between devices with their start and end apart: 86, of which 51 were waited for; matrix products, arithmetic and copies ran while one was open for 7% of the time, Pallas kernels for 24%

commit v1 on v0

--- a/solution.py
+++ b/solution.py
@@ -906,7 +906,7 @@
     def in_part(at, earlier):
         query_back(at, earlier or out_others)
         if at == 2:
-            earlier = feed_got
+            earlier = feed_got, out_got
         if at == 1:
             with jax.named_scope("out_grad"):
                 wide = after(branch_rows, earlier)
@@ -979,11 +979,9 @@
                 with jax.named_scope(name + "_grad"):
                     wide = after(normed_rows, sends)
                     _, got = other_shards(wide, groups, False)
-                    if name == "query_key":
-                        wide = after(wide, finish_early(late_own["value"]), gate_exchange)
                     late_own[name] = product_shard(wide, groups, ranks, rank, got, False)
                     last_exchange[name] = send_groups(late_own[name])
-            return late_own["value"]
+            return late_own["value"], finish_early(late_own["value"]), gate_exchange
 
         arrived, parts, in_steps = scatter_ring(in_part, lambda at, earlier: down_parts[at], hook=in_hook)
     with jax.named_scope("finish_rows"):

time: 429 us -> 429 us (level)
  transfers between devices with their start and end apart: 86 -> 86, of which waited for: 51 -> 53; matrix products, arithmetic and copies ran while one was open for 7% -> 7% of each run, Pallas kernels for 24% -> 24%
where the time goes in v1:
time: 429 us; the launch traced here: 422 us
  waiting for transfers between devices  196 us (46%)
  Pallas kernels  110 us (26%)
  starting transfers between devices  74.3 us (17%)
  other arithmetic  15.3 us (4%)
  local copies, waits for them, and re-layouts  13.1 us (3%)
  matrix products  9.38 us (2%)
    ppermute x56, waiting for transfers between devices, ring_shift(): return lax.ppermute(value, 'mp', pairs)  184 us
    pallas_call x28, Pallas kernels, run(): pl.pallas_call(kernel, out_shape=[jax.ShapeDtypeStruct(shape, dtype) for...  86.8 us
    ppermute x56, starting transfers between devices, ring_shift(): return lax.ppermute(value, 'mp', pairs)  59.5 us
    pallas_call x8, Pallas kernels, product_shard(): pl.pallas_call(kernel, grid_spec=pltpu.PrefetchScalarGridSpec(num_scalar_...  23.5 us
  transfers between devices with their start and end apart: 86, of which 53 were waited for; matrix products, arithmetic and copies ran while one was open for 7% of the time, Pallas kernels for 24%

profile of v1, /device:TPU:0, one launch (start us, length us, event | category | flops | bytes accessed | tf_op | source)
XLA Modules:
  0.0 421.9 jit_solution(1874242781132511035)
XLA Ops:
  0.7 3.0 collective-permute-start.1
  9.6 1.9 multiply_sine_fusion
  23.9 5.9 %collective-permute-done.2.refs_3_ = bf16[128,2048]{1,0:T(8,128)(2,1)S(1)} collective-permute-done((bf16[128,2048]{1,0:T(8,128)(2,1)S(1)}, bf16[128,2048]{1,0:T(8,128)(2,1)S(1)}, u32[]{:S(2)}, u32[]{:S(2)}) %collective-permute-start.2) | collective-permute-done | bytes 524320 | tf_op jit(solution)/shard_map/project_in/ppermute | solution.py:492
  31.8 1.6 collective-permute-start.8
  33.8 7.7 %project.3 = (bf16[640,2048]{1,0:T(8,128)(2,1)S(1)}, bf16[640,2048]{1,0:T(8,128)(2,1)S(1)}, bf16[640,1024]{1,0:T(8,128)(2,1)S(1)}, f32[640,512]{1,0:T(8,128)S(1)}, f32[640,2]{1,0:T(8,128)S(1)}) custom-call(bf16[128,2048]{1,0:T(8,128)(2,1)S(1)} %copy-done.44, bf16[128,2048]{1,0:T(8,128)(2,1)S(1)} %collective-permute-done.refs_1_, ...), custom_call_target="tpu_custom_call" | custom-call | flops 4026531840 | bytes 17454080 | tf_op jit(solution)/shard_map/project_in/project/pallas_call | solution.py:101
  41.7 4.4 %collective-permute-done.8.refs_0_ = bf16[128,2048]{1,0:T(8,128)(2,1)S(1)} collective-permute-done((bf16[128,2048]{1,0:T(8,128)(2,1)S(1)}, bf16[128,2048]{1,0:T(8,128)(2,1)S(1)}, u32[]{:S(2)}, u32[]{:S(2)}) %collective-permute-start.8) | collective-permute-done | bytes 524320 | tf_op jit(solution)/shard_map/project_in/ppermute | solution.py:492
  47.9 1.6 collective-permute-start.11
  50.1 3.5 project.4
  53.9 1.7 collective-permute-done.11.refs_0_
  57.0 2.1 project.5
  61.4 1.7 branch.3
  65.3 2.8 branch.4
  68.2 11.2 %collective-permute-done.16 = bf16[128,1024]{1,0:T(8,128)(2,1)S(1)} collective-permute-done((bf16[128,1024]{1,0:T(8,128)(2,1)S(1)}, bf16[128,1024]{1,0:T(8,128)(2,1)S(1)}, u32[]{:S(2)}, u32[]{:S(2)}) %collective-permute-start.16) | collective-permute-done | bytes 262176 | tf_op jit(solution)/shard_map/retention/ppermute | solution.py:492
  79.7 1.6 collective-permute-start.20
  81.8 6.0 %branch.5 = (bf16[128,2048]{1,0:T(8,128)(2,1)S(1)}, bf16[256,2048]{1,0:T(8,128)(2,1)S(1)}, bf16[256,2048]{1,0:T(8,128)(2,1)S(1)}, bf16[640,512]{1,0:T(8,128)(2,1...) custom-call(bf16[640,1024]{1,0:T(8,128)(2,1)S(1)} %get-tuple-element.530.refs_1_.refs_0_, ...), custom_call_target="tpu_custom_call" | custom-call | flops 3355443200 | bytes 13570560 | tf_op jit(solution)/shard_map/retention/branch/pallas_call | solution.py:101
  89.8 3.2 collective-permute-done.20
  99.2 10.4 %collective-permute-done.22 = bf16[128,2048]{1,0:T(8,128)(2,1)S(1)} collective-permute-done((bf16[128,2048]{1,0:T(8,128)(2,1)S(1)}, bf16[128,2048]{1,0:T(8,128)(2,1)S(1)}, u32[]{:S(2)}, u32[]{:S(2)}) %collective-permute-start.22) | collective-permute-done | bytes 524320 | tf_op jit(solution)/shard_map/retention/ppermute | solution.py:492
  114.4 6.5 %collective-permute-done.30.refs_8_ = bf16[128,2048]{1,0:T(8,128)(2,1)} collective-permute-done((bf16[128,2048]{1,0:T(8,128)(2,1)}, bf16[128,2048]{1,0:T(8,128)(2,1)}, u32[]{:S(2)}, u32[]{:S(2)}) %collective-permute-start.30) | collective-permute-done | bytes 524320 | tf_op jit(solution)/shard_map/gather_out_grad/ppermute | solution.py:492
  123.4 8.8 %collective-permute-done.24 = bf16[128,2048]{1,0:T(8,128)(2,1)} collective-permute-done((bf16[128,2048]{1,0:T(8,128)(2,1)}, bf16[128,2048]{1,0:T(8,128)(2,1)}, u32[]{:S(2)}, u32[]{:S(2)}) %collective-permute-start.24) | collective-permute-done | bytes 524320 | tf_op jit(solution)/shard_map/retention/ppermute | solution.py:492
  132.7 2.0 fusion.48
  137.6 15.3 %collective-permute-done.27.refs_2_ = bf16[128,2048]{1,0:T(8,128)(2,1)S(1)} collective-permute-done((bf16[128,2048]{1,0:T(8,128)(2,1)S(1)}, bf16[128,2048]{1,0:T(8,128)(2,1)S(1)}, u32[]{:S(2)}, u32[]{:S(2)}) %collective-permute-start.27) | collective-permute-done | bytes 524320 | tf_op jit(solution)/shard_map/feed_forward/ppermute | solution.py:492
  157.3 10.5 %collective-permute-done.28.refs_3_ = bf16[128,2048]{1,0:T(8,128)(2,1)S(1)} collective-permute-done((bf16[128,2048]{1,0:T(8,128)(2,1)S(1)}, bf16[128,2048]{1,0:T(8,128)(2,1)S(1)}, u32[]{:S(2)}, u32[]{:S(2)}) %collective-permute-start.28) | collective-permute-done | bytes 524320 | tf_op jit(solution)/shard_map/feed_forward/ppermute | solution.py:492
  171.1 2.3 collective-permute-done.40.refs_2_
  174.4 7.7 %feed.3 = (bf16[640,2048]{1,0:T(8,128)(2,1)S(1)}, bf16[640,2048]{1,0:T(8,128)(2,1)S(1)}, bf16[640,512]{1,0:T(8,128)(2,1)S(1)}, bf16[640,512]{1,0:T(8,128)(2,1)S(...) custom-call(bf16[128,2048]{1,0:T(8,128)(2,1)S(1)} %add_convert_fusion.6.refs_0_, ...), custom_call_target="tpu_custom_call" | custom-call | flops 4026531840 | bytes 18612224 | tf_op jit(solution)/shard_map/feed_forward/feed/pallas_call | solution.py:101
  184.3 3.0 feed.4
  189.4 2.6 feed.5
  196.3 2.2 collective-permute-done.42
  203.6 7.4 %collective-permute-done.47 = bf16[128,2048]{1,0:T(8,128)(2,1)S(1)} collective-permute-done((bf16[128,2048]{1,0:T(8,128)(2,1)S(1)}, bf16[128,2048]{1,0:T(8,128)(2,1)S(1)}, u32[]{:S(2)}, u32[]{:S(2)}) %collective-permute-start.47) | collective-permute-done | bytes 524320 | tf_op jit(solution)/shard_map/scatter_up/ppermute | solution.py:492
  214.0 2.3 down.1
  218.1 5.4 %collective-permute-done.49 = bf16[128,2048]{1,0:T(8,128)(2,1)S(1)} collective-permute-done((bf16[128,2048]{1,0:T(8,128)(2,1)S(1)}, bf16[128,2048]{1,0:T(8,128)(2,1)S(1)}, u32[]{:S(2)}, u32[]{:S(2)}) %collective-permute-start.49) | collective-permute-done | bytes 524320 | tf_op jit(solution)/shard_map/scatter_up/ppermute | solution.py:492
  228.0 5.6 %collective-permute-done.51 = bf16[128,2048]{1,0:T(8,128)(2,1)S(1)} collective-permute-done((bf16[128,2048]{1,0:T(8,128)(2,1)S(1)}, bf16[128,2048]{1,0:T(8,128)(2,1)S(1)}, u32[]{:S(2)}, u32[]{:S(2)}) %collective-permute-start.51) | collective-permute-done | bytes 524320 | tf_op jit(solution)/shard_map/scatter_up/ppermute | solution.py:492
  239.4 10.5 %collective-permute-done.54.refs_2_ = bf16[128,2048]{1,0:T(8,128)(2,1)S(1)} collective-permute-done((bf16[128,2048]{1,0:T(8,128)(2,1)S(1)}, bf16[128,2048]{1,0:T(8,128)(2,1)S(1)}, u32[]{:S(2)}, u32[]{:S(2)}) %collective-permute-start.54) | collective-permute-done | bytes 524320 | tf_op jit(solution)/shard_map/gate_back/ppermute | solution.py:492
  249.9 3.6 collective-permute-done.53.refs_1_
  253.8 1.7 collective-permute-start.56
  256.9 10.5 %collective-permute-done.55.refs_3_ = bf16[128,2048]{1,0:T(8,128)(2,1)S(1)} collective-permute-done((bf16[128,2048]{1,0:T(8,128)(2,1)S(1)}, bf16[128,2048]{1,0:T(8,128)(2,1)S(1)}, u32[]{:S(2)}, u32[]{:S(2)}) %collective-permute-start.55) | collective-permute-done | bytes 524320 | tf_op jit(solution)/shard_map/gate_back/ppermute | solution.py:492
  270.0 3.9 gate_back.3
  274.1 2.9 collective-permute-done.57.refs_0_
  278.3 1.8 collective-permute-start.60
  280.4 1.8 gate_back.4
  282.2 2.6 collective-permute-done.60.refs_0_
  284.7 1.7 collective-permute-done.61.refs_1_
  288.0 2.7 product_shard.8
  294.1 4.8 %key_back.3 = (bf16[128,256]{1,0:T(8,128)(2,1)}, bf16[128,256]{1,0:T(8,128)(2,1)S(1)}, bf16[128,512]{1,0:T(8,128)(2,1)S(1)}, f32[2,2048]{1,0:T(2,128)S(1)}, bf16...) custom-call(bf16[128,1024]{1,0:T(8,128)(2,1)S(1)} %get-tuple-element.491.refs_0_.refs_3_, ...), custom_call_target="tpu_custom_call" | custom-call | tf_op jit(solution)/shard_map/key_back/key_back/pallas_call | solution.py:101
  299.1 1.7 collective-permute-start.65
  301.6 2.7 product_shard.10
  306.1 5.1 %key_back.4 = (bf16[256,256]{1,0:T(8,128)(2,1)}, bf16[256,256]{1,0:T(8,128)(2,1)S(1)}, bf16[256,512]{1,0:T(8,128)(2,1)S(1)}, f32[2,2048]{1,0:T(2,128)S(1)}, bf16[256,2048]{1,0:T(8,128)(2,1)S(1)}) custom-call(bf16[256,1024]{1,0:T(8,128)(2,1)S(1)} %get-tuple-element.504.refs_2_.refs_0_, bf16[640,1024]{1,0:T(8,128)(2,1)S(1)} %get-tuple-element.530.refs_1_.refs_0_, ...), custom_call_target="tpu_custom_call" | custom-call | tf_op jit(solution)/shard_map/key_back/key_back/pallas_call | solution.py:101
  311.2 1.9 collective-permute-done.65.refs_0_
  313.1 1.8 collective-permute-done.66.refs_1_
  318.0 2.7 product_shard.9.refs_0_
  320.8 1.7 collective-permute-start.69
  322.5 3.4 query_back.5
  326.0 4.1 product_shard.11.refs_0_
  331.5 10.9 %key_back.5 = (bf16[640,256]{1,0:T(8,128)(2,1)}, bf16[640,256]{1,0:T(8,128)(2,1)S(1)}, bf16[640,512]{1,0:T(8,128)(2,1)S(1)}, f32[2,2048]{1,0:T(2,128)S(1)}, bf16...) custom-call(bf16[640,1024]{1,0:T(8,128)(2,1)S(1)} %get-tuple-element.530.refs_1_.refs_0_, ...), custom_call_target="tpu_custom_call" | custom-call | tf_op jit(solution)/shard_map/key_back/key_back/pallas_call | solution.py:101
  342.5 1.9 collective-permute-done.69.refs_1_
  344.9 2.7 product_shard.12
  351.4 3.0 product_shard.14
  354.5 2.7 product_shard.13.refs_0_
  359.3 2.7 finish_feed.1
  362.0 11.2 %collective-permute-done.71.refs_0_ = bf16[256,2048]{1,0:T(8,128)(2,1)S(1)} collective-permute-done((bf16[256,2048]{1,0:T(8,128)(2,1)S(1)}, bf16[256,2048]{1,0:T(8,128)(2,1)S(1)}, u32[]{:S(2)}, u32[]{:S(2)}) %collective-permute-start.71) | collective-permute-done | bytes 1048608 | tf_op jit(solution)/shard_map/key_back/ppermute | solution.py:492
  378.5 2.9 product_shard.15.refs_0_
  381.3 1.7 collective-permute-start.79
  383.1 16.3 %collective-permute-done.75.refs_0_ = bf16[256,2048]{1,0:T(8,128)(2,1)S(1)} collective-permute-done((bf16[256,2048]{1,0:T(8,128)(2,1)S(1)}, bf16[256,2048]{1,0:T(8,128)(2,1)S(1)}, u32[]{:S(2)}, u32[]{:S(2)}) %collective-permute-start.75) | collective-permute-done | bytes 1048608 | tf_op jit(solution)/shard_map/key_back/ppermute | solution.py:492
  400.5 2.2 finish_rows.1
  409.3 4.8 %collective-permute-done.84 = f32[4,2048]{1,0:T(4,128)S(1)} collective-permute-done((f32[4,2048]{1,0:T(4,128)S(1)}, f32[4,2048]{1,0:T(4,128)S(1)}, u32[]{:S(2)}, u32[]{:S(2)}) %collective-permute-start.84) | collective-permute-done | bytes 32800 | tf_op jit(solution)/shard_map/norm_grads/ppermute | solution.py:1017
  (515 shorter events, 129.8 us)
Async XLA Ops:
  0.7 15.2 %collective-permute-start.1 = (bf16[128,2048]{1,0:T(8,128)(2,1)}, bf16[128,2048]{1,0:T(8,128)(2,1)S(1)}, u32[]{:S(2)}, u32[]{:S(2)}) collective-permute-start(bf16[128,2048]{1,0:T(8,128)(2,1)} %refs_6_.1), channel_id=1, source_target_pairs={{0,2},{1,3},{4,0},{5,1},{8,4},{9,5},{12,8},{13,9},{14,12},{15,13},... | collective-permute-start | bytes 1572872 | tf_op jit(solution)/shard_map/project_in/ppermute | solution.py:492
  3.7 13.6 %collective-permute-start = (bf16[128,2048]{1,0:T(8,128)(2,1)}, bf16[128,2048]{1,0:T(8,128)(2,1)S(1)}, u32[]{:S(2)}, u32[]{:S(2)}) collective-permute-start(bf16[128,2048]{1,0:T(8,128)(2,1)} %refs_6_.1), channel_id=1, source_target_pairs={{0,4},{1,5},{4,8},{5,9},{8,12},{9,13},{12,14},{13,15},{14,10},{15,... | collective-permute-start | bytes 1572872 | tf_op jit(solution)/shard_map/project_in/ppermute | solution.py:492
  3.8 11.1 %collective-permute-start.4 = (bf16[2048,128]{1,0:T(8,128)(2,1)}, bf16[2048,128]{1,0:T(8,128)(2,1)}, u32[]{:S(2)}, u32[]{:S(2)}) collective-permute-start(bf16[2048,128]{1,0:T(8,128)(2,1)} %param.18), channel_id=1, source_target_pairs={{0,1},{1,0},{2,3},{3,2},{4,5},{5,4},{6,7},{7,6},{8,9},{9,8},{10,11... | collective-permute-start | bytes 1572872 | tf_op jit(solution)/shard_map/head_weights/ppermute | solution.py:496
  3.8 11.1 %collective-permute-start.5 = (bf16[2048,128]{1,0:T(8,128)(2,1)}, bf16[2048,128]{1,0:T(8,128)(2,1)}, u32[]{:S(2)}, u32[]{:S(2)}) collective-permute-start(bf16[2048,128]{1,0:T(8,128)(2,1)} %param.19), channel_id=1, source_target_pairs={{0,1},{1,0},{2,3},{3,2},{4,5},{5,4},{6,7},{7,6},{8,9},{9,8},{10,11... | collective-permute-start | bytes 1572872 | tf_op jit(solution)/shard_map/head_weights/ppermute | solution.py:496
  17.3 12.5 %collective-permute-start.2 = (bf16[128,2048]{1,0:T(8,128)(2,1)S(1)}, bf16[128,2048]{1,0:T(8,128)(2,1)S(1)}, u32[]{:S(2)}, u32[]{:S(2)}) collective-permute-start(bf16[128,2048]{1,0:T(8,128)(2,1)S(1)} %collective-permute-done.refs_1_), channel_id=1, source_target_pairs={{0,4},{1,5},{4,8},{5,9},{8,12},{9,13},{12,14},{13,15},{14,10},{15,... | collective-permute-start | bytes 1572872 | tf_op jit(solution)/shard_map/project_in/ppermute | solution.py:492
  17.7 12.8 %collective-permute-start.3 = (bf16[128,2048]{1,0:T(8,128)(2,1)S(1)}, bf16[128,2048]{1,0:T(8,128)(2,1)S(1)}, u32[]{:S(2)}, u32[]{:S(2)}) collective-permute-start(bf16[128,2048]{1,0:T(8,128)(2,1)S(1)} %collective-permute-done.1.refs_2_), channel_id=1, source_target_pairs={{0,2},{1,3},{4,0},{5,1},{8,4},{9,5},{12,8},{13,9},{14,12},{15,13},... | collective-permute-start | bytes 1572872 | tf_op jit(solution)/shard_map/project_in/ppermute | solution.py:492
  19.3 11.8 %collective-permute-start.7 = (bf16[2048,256]{1,0:T(8,128)(2,1)}, bf16[2048,256]{1,0:T(8,128)(2,1)S(1)}, u32[]{:S(2)}, u32[]{:S(2)}) collective-permute-start(bf16[2048,256]{1,0:T(8,128)(2,1)} %param.21), channel_id=1, source_target_pairs={{0,1},{1,0},{2,3},{3,2},{4,5},{5,4},{6,7},{7,6},{8,9},{9,8},{10,11... | collective-permute-start | bytes 3145736 | tf_op jit(solution)/shard_map/head_weights/ppermute | solution.py:496
  19.3 11.2 %collective-permute-start.6 = (bf16[2048,256]{1,0:T(8,128)(2,1)}, bf16[2048,256]{1,0:T(8,128)(2,1)S(1)}, u32[]{:S(2)}, u32[]{:S(2)}) collective-permute-start(bf16[2048,256]{1,0:T(8,128)(2,1)} %param.20), channel_id=1, source_target_pairs={{0,1},{1,0},{2,3},{3,2},{4,5},{5,4},{6,7},{7,6},{8,9},{9,8},{10,11... | collective-permute-start | bytes 3145736 | tf_op jit(solution)/shard_map/head_weights/ppermute | solution.py:496
  30.5 16.9 %collective-permute-start.10 = (bf16[256,2048]{1,0:T(8,128)(2,1)S(1)}, bf16[256,2048]{1,0:T(8,128)(2,1)S(1)}, u32[]{:S(2)}, u32[]{:S(2)}) collective-permute-start(bf16[256,2048]{1,0:T(8,128)(2,1)S(1)} %copy-done.120), channel_id=1, source_target_pairs={{0,1},{1,0},{2,3},{3,2},{4,5},{5,4},{6,7},{7,6},{8,9},{9,8},{10,11... | collective-permute-start | bytes 3145736 | tf_op jit(solution)/shard_map/head_weights/ppermute | solution.py:496
  31.8 14.4 %collective-permute-start.8 = (bf16[128,2048]{1,0:T(8,128)(2,1)S(1)}, bf16[128,2048]{1,0:T(8,128)(2,1)S(1)}, u32[]{:S(2)}, u32[]{:S(2)}) collective-permute-start(bf16[128,2048]{1,0:T(8,128)(2,1)S(1)} %collective-permute-done.2.refs_3_), channel_id=1, source_target_pairs={{0,4},{1,5},{4,8},{5,9},{8,12},{9,13},{12,14},{13,15},{14,10},{15,... | collective-permute-start | bytes 1572872 | tf_op jit(solution)/shard_map/project_in/ppermute | solution.py:492
  33.4 14.0 %collective-permute-start.9 = (bf16[128,2048]{1,0:T(8,128)(2,1)S(1)}, bf16[128,2048]{1,0:T(8,128)(2,1)S(1)}, u32[]{:S(2)}, u32[]{:S(2)}) collective-permute-start(bf16[128,2048]{1,0:T(8,128)(2,1)S(1)} %collective-permute-done.3.refs_4_), channel_id=1, source_target_pairs={{0,2},{1,3},{4,0},{5,1},{8,4},{9,5},{12,8},{13,9},{14,12},{15,13},... | collective-permute-start | bytes 1572872 | tf_op jit(solution)/shard_map/project_in/ppermute | solution.py:492
  59.3 22.5 %collective-permute-start.19 = (bf16[128,2048]{1,0:T(8,128)(2,1)S(1)}, bf16[128,2048]{1,0:T(8,128)(2,1)}, u32[]{:S(2)}, u32[]{:S(2)}) collective-permute-start(bf16[128,2048]{1,0:T(8,128)(2,1)S(1)} %copy-done.72), channel_id=1, source_target_pairs={{0,2},{1,3},{4,0},{5,1},{8,4},{9,5},{12,8},{13,9},{14,12},{15,13},... | collective-permute-start | bytes 1572872 | tf_op jit(solution)/shard_map/gather_out_grad/ppermute | solution.py:492
  59.8 22.0 %collective-permute-start.18 = (bf16[128,2048]{1,0:T(8,128)(2,1)S(1)}, bf16[128,2048]{1,0:T(8,128)(2,1)}, u32[]{:S(2)}, u32[]{:S(2)}) collective-permute-start(bf16[128,2048]{1,0:T(8,128)(2,1)S(1)} %copy-done.72), channel_id=1, source_target_pairs={{0,4},{1,5},{4,8},{5,9},{8,12},{9,13},{12,14},{13,15},{14,10},{15,... | collective-permute-start | bytes 1572872 | tf_op jit(solution)/shard_map/gather_out_grad/ppermute | solution.py:492
  63.2 16.2 %collective-permute-start.16 = (bf16[128,1024]{1,0:T(8,128)(2,1)S(1)}, bf16[128,1024]{1,0:T(8,128)(2,1)S(1)}, u32[]{:S(2)}, u32[]{:S(2)}) collective-permute-start(bf16[128,1024]{1,0:T(8,128)(2,1)S(1)} %get-tuple-element.340), channel_id=1, source_target_pairs={{0,4},{1,5},{4,8},{5,9},{8,12},{9,13},{12,14},{13,15},{14,10},{15,... | collective-permute-start | bytes 786440 | tf_op jit(solution)/shard_map/retention/ppermute | solution.py:492
  64.8 14.6 %collective-permute-start.17 = (bf16[128,1024]{1,0:T(8,128)(2,1)S(1)}, bf16[128,1024]{1,0:T(8,128)(2,1)S(1)}, u32[]{:S(2)}, u32[]{:S(2)}) collective-permute-start(bf16[128,1024]{1,0:T(8,128)(2,1)S(1)} %get-tuple-element.341), channel_id=1, source_target_pairs={{0,2},{1,3},{4,0},{5,1},{8,4},{9,5},{12,8},{13,9},{14,12},{15,13},... | collective-permute-start | bytes 786440 | tf_op jit(solution)/shard_map/retention/ppermute | solution.py:492
  79.7 13.4 %collective-permute-start.20 = (bf16[128,2048]{1,0:T(8,128)(2,1)S(1)}, bf16[128,2048]{1,0:T(8,128)(2,1)S(1)}, u32[]{:S(2)}, u32[]{:S(2)}) collective-permute-start(bf16[128,2048]{1,0:T(8,128)(2,1)S(1)} %pad_maximum_fusion.4), channel_id=1, source_target_pairs={{0,4},{1,5},{4,8},{5,9},{8,12},{9,13},{12,14},{13,15},{14,10},{15,... | collective-permute-start | bytes 1572872 | tf_op jit(solution)/shard_map/retention/ppermute | solution.py:492
  81.3 13.0 %collective-permute-start.21 = (bf16[128,2048]{1,0:T(8,128)(2,1)S(1)}, bf16[128,2048]{1,0:T(8,128)(2,1)S(1)}, u32[]{:S(2)}, u32[]{:S(2)}) collective-permute-start(bf16[128,2048]{1,0:T(8,128)(2,1)S(1)} %pad_maximum_fusion.5), channel_id=1, source_target_pairs={{0,2},{1,3},{4,0},{5,1},{8,4},{9,5},{12,8},{13,9},{14,12},{15,13},... | collective-permute-start | bytes 1572872 | tf_op jit(solution)/shard_map/retention/ppermute | solution.py:492
  94.7 14.9 %collective-permute-start.22 = (bf16[128,2048]{1,0:T(8,128)(2,1)S(1)}, bf16[128,2048]{1,0:T(8,128)(2,1)S(1)}, u32[]{:S(2)}, u32[]{:S(2)}) collective-permute-start(bf16[128,2048]{1,0:T(8,128)(2,1)S(1)} %get-tuple-element.359), channel_id=1, source_target_pairs={{0,4},{1,5},{4,8},{5,9},{8,12},{9,13},{12,14},{13,15},{14,10},{15,... | collective-permute-start | bytes 1572872 | tf_op jit(solution)/shard_map/retention/ppermute | solution.py:492
  96.2 14.9 %collective-permute-start.23 = (bf16[128,2048]{1,0:T(8,128)(2,1)S(1)}, bf16[128,2048]{1,0:T(8,128)(2,1)S(1)}, u32[]{:S(2)}, u32[]{:S(2)}) collective-permute-start(bf16[128,2048]{1,0:T(8,128)(2,1)S(1)} %get-tuple-element.360), channel_id=1, source_target_pairs={{0,2},{1,3},{4,0},{5,1},{8,4},{9,5},{12,8},{13,9},{14,12},{15,13},... | collective-permute-start | bytes 1572872 | tf_op jit(solution)/shard_map/retention/ppermute | solution.py:492
  96.8 24.2 %collective-permute-start.30 = (bf16[128,2048]{1,0:T(8,128)(2,1)}, bf16[128,2048]{1,0:T(8,128)(2,1)}, u32[]{:S(2)}, u32[]{:S(2)}) collective-permute-start(bf16[128,2048]{1,0:T(8,128)(2,1)} %collective-permute-done.18.refs_6_), channel_id=1, source_target_pairs={{0,4},{1,5},{4,8},{5,9},{8,12},{9,13},{12,14},{13,15},{14,10},{15,... | collective-permute-start | bytes 1572872 | tf_op jit(solution)/shard_map/gather_out_grad/ppermute | solution.py:492
  98.2 24.2 %collective-permute-start.31 = (bf16[128,2048]{1,0:T(8,128)(2,1)}, bf16[128,2048]{1,0:T(8,128)(2,1)}, u32[]{:S(2)}, u32[]{:S(2)}) collective-permute-start(bf16[128,2048]{1,0:T(8,128)(2,1)} %collective-permute-done.19.refs_7_), channel_id=1, source_target_pairs={{0,2},{1,3},{4,0},{5,1},{8,4},{9,5},{12,8},{13,9},{14,12},{15,13},... | collective-permute-start | bytes 1572872 | tf_op jit(solution)/shard_map/gather_out_grad/ppermute | solution.py:492
  112.4 19.8 %collective-permute-start.24 = (bf16[128,2048]{1,0:T(8,128)(2,1)}, bf16[128,2048]{1,0:T(8,128)(2,1)}, u32[]{:S(2)}, u32[]{:S(2)}) collective-permute-start(bf16[128,2048]{1,0:T(8,128)(2,1)} %get-tuple-element.363), channel_id=1, source_target_pairs={{0,4},{1,5},{4,8},{5,9},{8,12},{9,13},{12,14},{13,15},{14,10},{15,... | collective-permute-start | bytes 1572872 | tf_op jit(solution)/shard_map/retention/ppermute | solution.py:492
  113.4 19.3 %collective-permute-start.25 = (bf16[128,2048]{1,0:T(8,128)(2,1)}, bf16[128,2048]{1,0:T(8,128)(2,1)}, u32[]{:S(2)}, u32[]{:S(2)}) collective-permute-start(bf16[128,2048]{1,0:T(8,128)(2,1)} %get-tuple-element.364), channel_id=1, source_target_pairs={{0,2},{1,3},{4,0},{5,1},{8,4},{9,5},{12,8},{13,9},{14,12},{15,13},... | collective-permute-start | bytes 1572872 | tf_op jit(solution)/shard_map/retention/ppermute | solution.py:492
  114.4 21.3 %collective-permute-start.32 = (bf16[2048,256]{1,0:T(8,128)(2,1)}, bf16[2048,256]{1,0:T(8,128)(2,1)S(1)}, u32[]{:S(2)}, u32[]{:S(2)}) collective-permute-start(bf16[2048,256]{1,0:T(8,128)(2,1)} %param.23), channel_id=1, source_target_pairs={{0,1},{1,0},{2,3},{3,2},{4,5},{5,4},{6,7},{7,6},{8,9},{9,8},{10,11... | collective-permute-start | bytes 3145736 | tf_op jit(solution)/shard_map/feed_weights/ppermute | solution.py:496
  120.9 34.0 %collective-permute-start.33 = (bf16[256,2048]{1,0:T(8,128)(2,1)}, bf16[256,2048]{1,0:T(8,128)(2,1)S(1)}, u32[]{:S(2)}, u32[]{:S(2)}) collective-permute-start(bf16[256,2048]{1,0:T(8,128)(2,1)} %param.24), channel_id=1, source_target_pairs={{0,1},{1,0},{2,3},{3,2},{4,5},{5,4},{6,7},{7,6},{8,9},{9,8},{10,11... | collective-permute-start | bytes 3145736 | tf_op jit(solution)/shard_map/feed_weights/ppermute | solution.py:496
  122.4 32.7 %collective-permute-start.36 = (bf16[128,2048]{1,0:T(8,128)(2,1)}, bf16[128,2048]{1,0:T(8,128)(2,1)S(1)}, u32[]{:S(2)}, u32[]{:S(2)}) collective-permute-start(bf16[128,2048]{1,0:T(8,128)(2,1)} %collective-permute-done.30.refs_8_), channel_id=1, source_target_pairs={{0,4},{1,5},{4,8},{5,9},{8,12},{9,13},{12,14},{13,15},{14,10},{15,... | collective-permute-start | bytes 1572872 | tf_op jit(solution)/shard_map/gather_out_grad/ppermute | solution.py:492
  132.2 22.9 %collective-permute-start.37 = (bf16[128,2048]{1,0:T(8,128)(2,1)}, bf16[128,2048]{1,0:T(8,128)(2,1)S(1)}, u32[]{:S(2)}, u32[]{:S(2)}) collective-permute-start(bf16[128,2048]{1,0:T(8,128)(2,1)} %collective-permute-done.31.refs_9_), channel_id=1, source_target_pairs={{0,2},{1,3},{4,0},{5,1},{8,4},{9,5},{12,8},{13,9},{14,12},{15,13},... | collective-permute-start | bytes 1572872 | tf_op jit(solution)/shard_map/gather_out_grad/ppermute | solution.py:492
  135.2 17.7 %collective-permute-start.27 = (bf16[128,2048]{1,0:T(8,128)(2,1)S(1)}, bf16[128,2048]{1,0:T(8,128)(2,1)S(1)}, u32[]{:S(2)}, u32[]{:S(2)}) collective-permute-start(bf16[128,2048]{1,0:T(8,128)(2,1)S(1)} %add_convert_fusion.6.refs_0_), channel_id=1, source_target_pairs={{0,2},{1,3},{4,0},{5,1},{8,4},{9,5},{12,8},{13,9},{14,12},{15,13},... | collective-permute-start | bytes 1572872 | tf_op jit(solution)/shard_map/feed_forward/ppermute | solution.py:492
  135.7 17.2 %collective-permute-start.26 = (bf16[128,2048]{1,0:T(8,128)(2,1)S(1)}, bf16[128,2048]{1,0:T(8,128)(2,1)S(1)}, u32[]{:S(2)}, u32[]{:S(2)}) collective-permute-start(bf16[128,2048]{1,0:T(8,128)(2,1)S(1)} %add_convert_fusion.6.refs_0_), channel_id=1, source_target_pairs={{0,4},{1,5},{4,8},{5,9},{8,12},{9,13},{12,14},{13,15},{14,10},{15,... | collective-permute-start | bytes 1572872 | tf_op jit(solution)/shard_map/feed_forward/ppermute | solution.py:492
  152.9 14.9 %collective-permute-start.28 = (bf16[128,2048]{1,0:T(8,128)(2,1)S(1)}, bf16[128,2048]{1,0:T(8,128)(2,1)S(1)}, u32[]{:S(2)}, u32[]{:S(2)}) collective-permute-start(bf16[128,2048]{1,0:T(8,128)(2,1)S(1)} %collective-permute-done.26.refs_1_), channel_id=1, source_target_pairs={{0,4},{1,5},{4,8},{5,9},{8,12},{9,13},{12,14},{13,15},{14,10},{15,... | collective-permute-start | bytes 1572872 | tf_op jit(solution)/shard_map/feed_forward/ppermute | solution.py:492
  154.0 14.9 %collective-permute-start.29 = (bf16[128,2048]{1,0:T(8,128)(2,1)S(1)}, bf16[128,2048]{1,0:T(8,128)(2,1)S(1)}, u32[]{:S(2)}, u32[]{:S(2)}) collective-permute-start(bf16[128,2048]{1,0:T(8,128)(2,1)S(1)} %collective-permute-done.27.refs_2_), channel_id=1, source_target_pairs={{0,2},{1,3},{4,0},{5,1},{8,4},{9,5},{12,8},{13,9},{14,12},{15,13},... | collective-permute-start | bytes 1572872 | tf_op jit(solution)/shard_map/feed_forward/ppermute | solution.py:492
  155.2 18.2 %collective-permute-start.40 = (bf16[128,1024]{1,0:T(8,128)(2,1)S(1)}, bf16[128,1024]{1,0:T(8,128)(2,1)S(1)}, u32[]{:S(2)}, u32[]{:S(2)}) collective-permute-start(bf16[128,1024]{1,0:T(8,128)(2,1)S(1)} %slice.170), channel_id=1, source_target_pairs={{0,4},{1,5},{4,8},{5,9},{8,12},{9,13},{12,14},{13,15},{14,10},{15,... | collective-permute-start | bytes 786440 | tf_op jit(solution)/shard_map/gather_out_grad/ppermute | solution.py:492
  156.3 18.2 %collective-permute-start.41 = (bf16[128,1024]{1,0:T(8,128)(2,1)S(1)}, bf16[128,1024]{1,0:T(8,128)(2,1)S(1)}, u32[]{:S(2)}, u32[]{:S(2)}) collective-permute-start(bf16[128,1024]{1,0:T(8,128)(2,1)S(1)} %slice.171), channel_id=1, source_target_pairs={{0,2},{1,3},{4,0},{5,1},{8,4},{9,5},{12,8},{13,9},{14,12},{15,13},... | collective-permute-start | bytes 786440 | tf_op jit(solution)/shard_map/gather_out_grad/ppermute | solution.py:492
  168.8 13.4 %collective-permute-start.34 = (bf16[128,2048]{1,0:T(8,128)(2,1)S(1)}, bf16[128,2048]{1,0:T(8,128)(2,1)S(1)}, u32[]{:S(2)}, u32[]{:S(2)}) collective-permute-start(bf16[128,2048]{1,0:T(8,128)(2,1)S(1)} %collective-permute-done.28.refs_3_), channel_id=1, source_target_pairs={{0,4},{1,5},{4,8},{5,9},{8,12},{9,13},{12,14},{13,15},{14,10},{15,... | collective-permute-start | bytes 1572872 | tf_op jit(solution)/shard_map/feed_forward/ppermute | solution.py:492
  169.4 12.8 %collective-permute-start.35 = (bf16[128,2048]{1,0:T(8,128)(2,1)S(1)}, bf16[128,2048]{1,0:T(8,128)(2,1)S(1)}, u32[]{:S(2)}, u32[]{:S(2)}) collective-permute-start(bf16[128,2048]{1,0:T(8,128)(2,1)S(1)} %collective-permute-done.29.refs_4_), channel_id=1, source_target_pairs={{0,2},{1,3},{4,0},{5,1},{8,4},{9,5},{12,8},{13,9},{14,12},{15,13},... | collective-permute-start | bytes 1572872 | tf_op jit(solution)/shard_map/feed_forward/ppermute | solution.py:492
  196.2 20.2 %collective-permute-start.45 = (bf16[2048,256]{1,0:T(8,128)(2,1)S(1)}, bf16[2048,256]{1,0:T(8,128)(2,1)S(1)}, u32[]{:S(2)}, u32[]{:S(2)}) collective-permute-start(bf16[2048,256]{1,0:T(8,128)(2,1)S(1)} %convolution_convert_fusion), channel_id=1, source_target_pairs={{0,1},{1,0},{2,3},{3,2},{4,5},{5,4},{6,7},{7,6},{8,9},{9,8},{10,11... | collective-permute-start | bytes 3145736 | tf_op jit(solution)/shard_map/scatter_up/down_grad/ppermute | solution.py:496
  199.5 11.5 %collective-permute-start.47 = (bf16[128,2048]{1,0:T(8,128)(2,1)S(1)}, bf16[128,2048]{1,0:T(8,128)(2,1)S(1)}, u32[]{:S(2)}, u32[]{:S(2)}) collective-permute-start(bf16[128,2048]{1,0:T(8,128)(2,1)S(1)} %pad_maximum_fusion.6), channel_id=1, source_target_pairs={{0,4},{1,5},{4,8},{5,9},{8,12},{9,13},{12,14},{13,15},{14,10},{15,... | collective-permute-start | bytes 1572872 | tf_op jit(solution)/shard_map/scatter_up/ppermute | solution.py:492
  200.1 11.4 %collective-permute-start.48 = (bf16[128,2048]{1,0:T(8,128)(2,1)S(1)}, bf16[128,2048]{1,0:T(8,128)(2,1)S(1)}, u32[]{:S(2)}, u32[]{:S(2)}) collective-permute-start(bf16[128,2048]{1,0:T(8,128)(2,1)S(1)} %pad_maximum_fusion.7), channel_id=1, source_target_pairs={{0,2},{1,3},{4,0},{5,1},{8,4},{9,5},{12,8},{13,9},{14,12},{15,13},... | collective-permute-start | bytes 1572872 | tf_op jit(solution)/shard_map/scatter_up/ppermute | solution.py:492
  203.5 22.9 %collective-permute-start.44 = (bf16[2048,256]{1,0:T(8,128)(2,1)S(1)}, bf16[2048,256]{1,0:T(8,128)(2,1)S(1)}, u32[]{:S(2)}, u32[]{:S(2)}) collective-permute-start(bf16[2048,256]{1,0:T(8,128)(2,1)S(1)} %convolution_convert_fusion.1), channel_id=1, source_target_pairs={{0,1},{1,0},{2,3},{3,2},{4,5},{5,4},{6,7},{7,6},{8,9},{9,8},{10,11... | collective-permute-start | bytes 3145736 | tf_op jit(solution)/shard_map/scatter_up/up_grad/ppermute | solution.py:496
  211.9 11.7 %collective-permute-start.49 = (bf16[128,2048]{1,0:T(8,128)(2,1)S(1)}, bf16[128,2048]{1,0:T(8,128)(2,1)S(1)}, u32[]{:S(2)}, u32[]{:S(2)}) collective-permute-start(bf16[128,2048]{1,0:T(8,128)(2,1)S(1)} %get-tuple-element.438), channel_id=1, source_target_pairs={{0,4},{1,5},{4,8},{5,9},{8,12},{9,13},{12,14},{13,15},{14,10},{15,... | collective-permute-start | bytes 1572872 | tf_op jit(solution)/shard_map/scatter_up/ppermute | solution.py:492
  212.6 11.4 %collective-permute-start.50 = (bf16[128,2048]{1,0:T(8,128)(2,1)S(1)}, bf16[128,2048]{1,0:T(8,128)(2,1)S(1)}, u32[]{:S(2)}, u32[]{:S(2)}) collective-permute-start(bf16[128,2048]{1,0:T(8,128)(2,1)S(1)} %get-tuple-element.439), channel_id=1, source_target_pairs={{0,2},{1,3},{4,0},{5,1},{8,4},{9,5},{12,8},{13,9},{14,12},{15,13},... | collective-permute-start | bytes 1572872 | tf_op jit(solution)/shard_map/scatter_up/ppermute | solution.py:492
  224.4 9.2 %collective-permute-start.51 = (bf16[128,2048]{1,0:T(8,128)(2,1)S(1)}, bf16[128,2048]{1,0:T(8,128)(2,1)S(1)}, u32[]{:S(2)}, u32[]{:S(2)}) collective-permute-start(bf16[128,2048]{1,0:T(8,128)(2,1)S(1)} %get-tuple-element.442), channel_id=1, source_target_pairs={{0,4},{1,5},{4,8},{5,9},{8,12},{9,13},{12,14},{13,15},{14,10},{15,... | collective-permute-start | bytes 1572872 | tf_op jit(solution)/shard_map/scatter_up/ppermute | solution.py:492
  225.0 9.6 %collective-permute-start.52 = (bf16[128,2048]{1,0:T(8,128)(2,1)S(1)}, bf16[128,2048]{1,0:T(8,128)(2,1)S(1)}, u32[]{:S(2)}, u32[]{:S(2)}) collective-permute-start(bf16[128,2048]{1,0:T(8,128)(2,1)S(1)} %get-tuple-element.443), channel_id=1, source_target_pairs={{0,2},{1,3},{4,0},{5,1},{8,4},{9,5},{12,8},{13,9},{14,12},{15,13},... | collective-permute-start | bytes 1572872 | tf_op jit(solution)/shard_map/scatter_up/ppermute | solution.py:492
  237.4 12.5 %collective-permute-start.54 = (bf16[128,2048]{1,0:T(8,128)(2,1)S(1)}, bf16[128,2048]{1,0:T(8,128)(2,1)S(1)}, u32[]{:S(2)}, u32[]{:S(2)}) collective-permute-start(bf16[128,2048]{1,0:T(8,128)(2,1)S(1)} %get-tuple-element.460.refs_0_), channel_id=1, source_target_pairs={{0,2},{1,3},{4,0},{5,1},{8,4},{9,5},{12,8},{13,9},{14,12},{15,13},... | collective-permute-start | bytes 1572872 | tf_op jit(solution)/shard_map/gate_back/ppermute | solution.py:492
  238.9 14.5 %collective-permute-start.53 = (bf16[128,2048]{1,0:T(8,128)(2,1)S(1)}, bf16[128,2048]{1,0:T(8,128)(2,1)S(1)}, u32[]{:S(2)}, u32[]{:S(2)}) collective-permute-start(bf16[128,2048]{1,0:T(8,128)(2,1)S(1)} %get-tuple-element.460.refs_0_), channel_id=1, source_target_pairs={{0,4},{1,5},{4,8},{5,9},{8,12},{9,13},{12,14},{13,15},{14,10},{15,... | collective-permute-start | bytes 1572872 | tf_op jit(solution)/shard_map/gate_back/ppermute | solution.py:492
  253.4 13.9 %collective-permute-start.55 = (bf16[128,2048]{1,0:T(8,128)(2,1)S(1)}, bf16[128,2048]{1,0:T(8,128)(2,1)S(1)}, u32[]{:S(2)}, u32[]{:S(2)}) collective-permute-start(bf16[128,2048]{1,0:T(8,128)(2,1)S(1)} %collective-permute-done.53.refs_1_), channel_id=1, source_target_pairs={{0,4},{1,5},{4,8},{5,9},{8,12},{9,13},{12,14},{13,15},{14,10},{15,... | collective-permute-start | bytes 1572872 | tf_op jit(solution)/shard_map/gate_back/ppermute | solution.py:492
  253.8 14.0 %collective-permute-start.56 = (bf16[128,2048]{1,0:T(8,128)(2,1)S(1)}, bf16[128,2048]{1,0:T(8,128)(2,1)S(1)}, u32[]{:S(2)}, u32[]{:S(2)}) collective-permute-start(bf16[128,2048]{1,0:T(8,128)(2,1)S(1)} %collective-permute-done.54.refs_2_), channel_id=1, source_target_pairs={{0,2},{1,3},{4,0},{5,1},{8,4},{9,5},{12,8},{13,9},{14,12},{15,13},... | collective-permute-start | bytes 1572872 | tf_op jit(solution)/shard_map/gate_back/ppermute | solution.py:492
  255.5 37.3 %collective-permute-start.46 = (bf16[2048,512]{1,0:T(8,128)(2,1)S(1)}, bf16[2048,512]{1,0:T(8,128)(2,1)S(1)}, u32[]{:S(2)}, u32[]{:S(2)}) collective-permute-start(bf16[2048,512]{1,0:T(8,128)(2,1)S(1)} %pad_maximum_fusion.3.refs_0_), channel_id=1, source_target_pairs={{0,16},{16,0},{1,17},{17,1},{2,18},{18,2},{3,19},{19,3},{4,20},{20... | collective-permute-start | bytes 6291464 | tf_op jit(solution)/shard_map/feed_grads/ppermute | solution.py:761
  267.7 9.2 %collective-permute-start.57 = (bf16[128,2048]{1,0:T(8,128)(2,1)S(1)}, bf16[128,2048]{1,0:T(8,128)(2,1)S(1)}, u32[]{:S(2)}, u32[]{:S(2)}) collective-permute-start(bf16[128,2048]{1,0:T(8,128)(2,1)S(1)} %collective-permute-done.55.refs_3_), channel_id=1, source_target_pairs={{0,4},{1,5},{4,8},{5,9},{8,12},{9,13},{12,14},{13,15},{14,10},{15,... | collective-permute-start | bytes 1572872 | tf_op jit(solution)/shard_map/gate_back/ppermute | solution.py:492
  268.8 9.4 %collective-permute-start.58 = (bf16[128,2048]{1,0:T(8,128)(2,1)S(1)}, bf16[128,2048]{1,0:T(8,128)(2,1)S(1)}, u32[]{:S(2)}, u32[]{:S(2)}) collective-permute-start(bf16[128,2048]{1,0:T(8,128)(2,1)S(1)} %collective-permute-done.56.refs_4_), channel_id=1, source_target_pairs={{0,2},{1,3},{4,0},{5,1},{8,4},{9,5},{12,8},{13,9},{14,12},{15,13},... | collective-permute-start | bytes 1572872 | tf_op jit(solution)/shard_map/gate_back/ppermute | solution.py:492
  299.1 14.0 %collective-permute-start.65 = (bf16[256,1024]{1,0:T(8,128)(2,1)S(1)}, bf16[256,1024]{1,0:T(8,128)(2,1)S(1)}, u32[]{:S(2)}, u32[]{:S(2)}) collective-permute-start(bf16[256,1024]{1,0:T(8,128)(2,1)S(1)} %pad_maximum_fusion.8), channel_id=1, source_target_pairs={{0,4},{1,5},{4,8},{5,9},{8,12},{9,13},{12,14},{13,15},{14,10},{15,... | collective-permute-start | bytes 1572872 | tf_op jit(solution)/shard_map/key_back/ppermute | solution.py:492
  300.8 14.1 %collective-permute-start.66 = (bf16[256,1024]{1,0:T(8,128)(2,1)S(1)}, bf16[256,1024]{1,0:T(8,128)(2,1)S(1)}, u32[]{:S(2)}, u32[]{:S(2)}) collective-permute-start(bf16[256,1024]{1,0:T(8,128)(2,1)S(1)} %pad_maximum_fusion.9), channel_id=1, source_target_pairs={{0,2},{1,3},{4,0},{5,1},{8,4},{9,5},{12,8},{13,9},{14,12},{15,13},... | collective-permute-start | bytes 1572872 | tf_op jit(solution)/shard_map/key_back/ppermute | solution.py:492
  304.3 21.6 %collective-permute-start.70 = (bf16[2048,256]{1,0:T(8,128)(2,1)S(1)}, bf16[2048,256]{1,0:T(8,128)(2,1)}, u32[]{:S(2)}, u32[]{:S(2)}) collective-permute-start(bf16[2048,256]{1,0:T(8,128)(2,1)S(1)} %product_shard.10), channel_id=1, source_target_pairs={{0,1},{1,0},{2,3},{3,2},{4,5},{5,4},{6,7},{7,6},{8,9},{9,8},{10,11... | collective-permute-start | bytes 3145736 | tf_op jit(solution)/shard_map/key_back/gate_grad/ppermute | solution.py:496
  316.0 26.4 %collective-permute-start.67 = (bf16[256,2048]{1,0:T(8,128)(2,1)}, bf16[256,2048]{1,0:T(8,128)(2,1)S(1)}, u32[]{:S(2)}, u32[]{:S(2)}) collective-permute-start(bf16[256,2048]{1,0:T(8,128)(2,1)} %get-tuple-element.511), channel_id=1, source_target_pairs={{0,4},{1,5},{4,8},{5,9},{8,12},{9,13},{12,14},{13,15},{14,10},{15,... | collective-permute-start | bytes 3145736 | tf_op jit(solution)/shard_map/key_back/ppermute | solution.py:492
  317.3 25.2 %collective-permute-start.68 = (bf16[256,2048]{1,0:T(8,128)(2,1)S(1)}, bf16[256,2048]{1,0:T(8,128)(2,1)S(1)}, u32[]{:S(2)}, u32[]{:S(2)}) collective-permute-start(bf16[256,2048]{1,0:T(8,128)(2,1)S(1)} %get-tuple-element.512), channel_id=1, source_target_pairs={{0,2},{1,3},{4,0},{5,1},{8,4},{9,5},{12,8},{13,9},{14,12},{15,13},... | collective-permute-start | bytes 3145736 | tf_op jit(solution)/shard_map/key_back/ppermute | solution.py:492
  320.8 23.6 %collective-permute-start.69 = (bf16[256,2048]{1,0:T(8,128)(2,1)S(1)}, bf16[256,2048]{1,0:T(8,128)(2,1)S(1)}, u32[]{:S(2)}, u32[]{:S(2)}) collective-permute-start(bf16[256,2048]{1,0:T(8,128)(2,1)S(1)} %product_shard.9.refs_0_), channel_id=1, source_target_pairs={{0,16},{16,0},{1,17},{17,1},{2,18},{18,2},{3,19},{19,3},{4,20},{20... | collective-permute-start | bytes 3145736 | tf_op jit(solution)/shard_map/key_back/out_grad/ppermute | solution.py:761
  347.7 25.6 %collective-permute-start.71 = (bf16[256,2048]{1,0:T(8,128)(2,1)S(1)}, bf16[256,2048]{1,0:T(8,128)(2,1)S(1)}, u32[]{:S(2)}, u32[]{:S(2)}) collective-permute-start(bf16[256,2048]{1,0:T(8,128)(2,1)S(1)} %get-tuple-element.536), channel_id=1, source_target_pairs={{0,4},{1,5},{4,8},{5,9},{8,12},{9,13},{12,14},{13,15},{14,10},{15,... | collective-permute-start | bytes 3145736 | tf_op jit(solution)/shard_map/key_back/ppermute | solution.py:492
  349.0 25.2 %collective-permute-start.72 = (bf16[256,2048]{1,0:T(8,128)(2,1)S(1)}, bf16[256,2048]{1,0:T(8,128)(2,1)S(1)}, u32[]{:S(2)}, u32[]{:S(2)}) collective-permute-start(bf16[256,2048]{1,0:T(8,128)(2,1)S(1)} %get-tuple-element.537), channel_id=1, source_target_pairs={{0,2},{1,3},{4,0},{5,1},{8,4},{9,5},{12,8},{13,9},{14,12},{15,13},... | collective-permute-start | bytes 3145736 | tf_op jit(solution)/shard_map/key_back/ppermute | solution.py:492
  349.8 26.0 %collective-permute-start.74 = (bf16[2048,256]{1,0:T(8,128)(2,1)S(1)}, bf16[2048,256]{1,0:T(8,128)(2,1)S(1)}, u32[]{:S(2)}, u32[]{:S(2)}) collective-permute-start(bf16[2048,256]{1,0:T(8,128)(2,1)S(1)} %product_shard.11.refs_0_), channel_id=1, source_target_pairs={{0,16},{16,0},{1,17},{17,1},{2,18},{18,2},{3,19},{19,3},{4,20},{20... | collective-permute-start | bytes 3145736 | tf_op jit(solution)/shard_map/key_back/ppermute | solution.py:761
  354.4 24.0 %collective-permute-start.78 = (bf16[2048,256]{1,0:T(8,128)(2,1)S(1)}, bf16[2048,256]{1,0:T(8,128)(2,1)S(1)}, u32[]{:S(2)}, u32[]{:S(2)}) collective-permute-start(bf16[2048,256]{1,0:T(8,128)(2,1)S(1)} %product_shard.14), channel_id=1, source_target_pairs={{0,1},{1,0},{2,3},{3,2},{4,5},{5,4},{6,7},{7,6},{8,9},{9,8},{10,11... | collective-permute-start | bytes 3145736 | tf_op jit(solution)/shard_map/key_back/query_key_grad/ppermute | solution.py:496
  357.3 43.1 %collective-permute-start.77 = (bf16[2048,256]{1,0:T(8,128)(2,1)S(1)}, bf16[2048,256]{1,0:T(8,128)(2,1)S(1)}, u32[]{:S(2)}, u32[]{:S(2)}) collective-permute-start(bf16[2048,256]{1,0:T(8,128)(2,1)S(1)} %product_shard.13.refs_0_), channel_id=1, source_target_pairs={{0,16},{16,0},{1,17},{17,1},{2,18},{18,2},{3,19},{19,3},{4,20},{20... | collective-permute-start | bytes 3145736 | tf_op jit(solution)/shard_map/key_back/value_grad/ppermute | solution.py:761
  376.4 23.0 %collective-permute-start.75 = (bf16[256,2048]{1,0:T(8,128)(2,1)S(1)}, bf16[256,2048]{1,0:T(8,128)(2,1)S(1)}, u32[]{:S(2)}, u32[]{:S(2)}) collective-permute-start(bf16[256,2048]{1,0:T(8,128)(2,1)S(1)} %get-tuple-element.553), channel_id=1, source_target_pairs={{0,4},{1,5},{4,8},{5,9},{8,12},{9,13},{12,14},{13,15},{14,10},{15,... | collective-permute-start | bytes 3145736 | tf_op jit(solution)/shard_map/key_back/ppermute | solution.py:492
  377.7 22.7 %collective-permute-start.76 = (bf16[256,2048]{1,0:T(8,128)(2,1)S(1)}, bf16[256,2048]{1,0:T(8,128)(2,1)S(1)}, u32[]{:S(2)}, u32[]{:S(2)}) collective-permute-start(bf16[256,2048]{1,0:T(8,128)(2,1)S(1)} %get-tuple-element.554), channel_id=1, source_target_pairs={{0,2},{1,3},{4,0},{5,1},{8,4},{9,5},{12,8},{13,9},{14,12},{15,13},... | collective-permute-start | bytes 3145736 | tf_op jit(solution)/shard_map/key_back/ppermute | solution.py:492
  381.3 38.3 %collective-permute-start.79 = (bf16[2048,256]{1,0:T(8,128)(2,1)S(1)}, bf16[2048,256]{1,0:T(8,128)(2,1)S(1)}, u32[]{:S(2)}, u32[]{:S(2)}) collective-permute-start(bf16[2048,256]{1,0:T(8,128)(2,1)S(1)} %product_shard.15.refs_0_), channel_id=1, source_target_pairs={{0,16},{16,0},{1,17},{17,1},{2,18},{18,2},{3,19},{19,3},{4,20},{20... | collective-permute-start | bytes 3145736 | tf_op jit(solution)/shard_map/key_back/query_key_grad/ppermute | solution.py:761
  (155 other events, 1833.0 us)
